TPU v7x, 256 devices: a whole 4x4x8 slice. The times are simulated.
256 devices in a mesh: gx: 8 (over x, core), gy: 16 (over y_hi, z), gz: 2 (over y_lo).
Axes of the slice: x: 4, y: 4 (y_hi: 2, y_lo: 2; y = y_hi * 2 + y_lo), z: 8, core: 2. Of those that a mesh axis runs over, the one named last changes fastest.
Arguments:
- fields: float32 [4, 64, 512, 256], P(None, 'gx', 'gy', 'gz'), may hold values from -6 to 6
- viscosity: float32 [64, 512, 256], P('gx', 'gy', 'gz'), may hold values from 0.02 to 0.6
- samples: int32 [8, 16, 2, 8], P('gx', 'gy', 'gz'), may hold values from 0 to 511
- trainers: int32 [8, 16, 2, 8, 1], P('gx', 'gy', 'gz'), may hold values from 0 to 15; in each aligned block of 8 rows (0 to 7, 8 to 15, ..., all dimensions but the last counted through in order) at most 2 rows name the same one
- conv_first: bfloat16 [32, 108], replicated, may hold values from -0.625 to 0.625
- conv_second: bfloat16 [32, 864], replicated, may hold values from -0.21875 to 0.21875
- conv_third: bfloat16 [6, 32], replicated, may hold values from -1 to 1
Outputs:
- advanced: float32 [4, 64, 512, 256], P(None, 'gx', 'gy', 'gz')
- block_losses: float32 [8, 16, 2, 32], P('gx', 'gy', 'gz')
- first_grad: float32 [32, 108], replicated
- second_grad: float32 [32, 864], replicated
- third_grad: float32 [6, 32], replicated
Inputs may be any that keep to these rules, and one draw needn't show every extreme that they name: `trainers`: among the 8 samples of one device no trainer occurs more than 2 times, and on some device one occurs exactly 2 times.
All inputs are finite; a program needn't handle non-finite values.
Results may differ from a plain program's by a relative error of at most 0.0036.
The roundings to bfloat16 on the way count: a program that leaves them out, or rounds other values in their place, can miss the bound.
Values may be sent and summed in bfloat16 or wider, within the bound.
A program may use at most 128 MiB of HBM per device.

v0:
```python
import jax
import jax.numpy as jnp
from jax import lax
from jax.experimental import pallas as pl
from jax.experimental.pallas import tpu as pltpu
from jax.sharding import PartitionSpec as P

MESH = pl.DeviceIdType.MESH
F32 = jnp.float32
BF16 = jnp.bfloat16
I32 = jnp.int32
HIGH = lax.Precision.HIGHEST

NX, NY, NZ = 8, 16, 2
WORKERS = NX * NY * NZ
NT = (((1,), (1,)), ((), ()))
TN = (((0,), (0,)), ((), ()))
TIME_STEP = 0.25
BUOYANCY = 0.5
PAIR_P = (0, 1, 2, 0, 0, 1)
PAIR_Q = (0, 1, 2, 1, 2, 2)


def iota(shape, dim):
    return lax.broadcasted_iota(I32, shape, dim)


def flux(low, high, visc_low, visc_high, d):
    speed = 0.25 * (low[d] + high[d])
    visc = 0.5 * (visc_low + visc_high)
    return [speed * (a + b) - visc * (b - a) for a, b in zip(low, high)]


def advance_plane(src, visc, halo_y, visc_y, halo_z, p):
    rows = iota((32, 128), 0)
    lanes = iota((32, 128), 1)
    q = [src[c, p] for c in range(4)]
    v = visc(p)
    q_before = [src[c, p - 1] for c in range(4)]
    q_after = [src[c, p + 1] for c in range(4)]
    total = [
        a - b
        for a, b in zip(flux(q, q_after, v, visc(p + 1), 0), flux(q_before, q, visc(p - 1), v, 0))
    ]
    at = pl.ds(p - 1, 1)
    y_low = [halo_y[0, c, at] for c in range(4)]
    y_high = [halo_y[1, c, at] for c in range(4)]

    def up(x, edge):
        return jnp.where(rows == 31, edge, pltpu.roll(x, 31, 0))

    q_next = [up(x, e) for x, e in zip(q, y_high)]
    faces = flux(q, q_next, v, up(v, visc_y[1, 4, at]), 1)
    first = flux(y_low, [x[0:1] for x in q], visc_y[0, 4, at], v[0:1], 1)
    total = [
        t + (f - jnp.where(rows == 0, e, pltpu.roll(f, 1, 0)))
        for t, f, e in zip(total, faces, first)
    ]
    side = [halo_z[c, p - 1] for c in range(4)]
    side_v = halo_z[4, p - 1]

    def along(x, edge):
        return jnp.where(lanes == 127, edge, pltpu.roll(x, 127, 1))

    q_next = [along(x, e) for x, e in zip(q, side)]
    faces = flux(q, q_next, v, along(v, side_v), 2)
    first = flux(side, q, side_v, v, 2)
    total = [
        t + (f - jnp.where(lanes == 0, e, pltpu.roll(f, 1, 1)))
        for t, f, e in zip(total, faces, first)
    ]
    out = [x - TIME_STEP * t for x, t in zip(q, total)]
    out[2] = out[2] + (TIME_STEP * BUOYANCY) * q[3]
    return out


def pack_sides(src, count, y_send, z_send):
    for c in range(count):
        y_send[0, c] = src[c, 1:9, 0, :]
        y_send[1, c] = src[c, 1:9, 31, :]
        for h in range(2):
            turned = src[c, 1 + 4 * h : 5 + 4 * h].reshape(128, 128).T
            g = 2 * c + h
            z_send[0, g : g + 1, :] = turned[0:1]
            z_send[1, g : g + 1, :] = turned[127:128]


def unpack_sides(z_recv, count, halo_z):
    rows = iota((128, 128), 0)
    for c in range(count):
        for h in range(2):
            g = 2 * c + h
            first = z_recv[0, g : g + 1, :]
            last = z_recv[1, g : g + 1, :]
            placed = jnp.where(rows == 0, last, jnp.where(rows == 127, first, 0.0))
            halo_z[c, 4 * h : 4 * h + 4] = placed.T.reshape(4, 32, 128)


def by_lane(values, lanes_of):
    out = jnp.zeros(lanes_of.shape, I32)
    for j in range(8):
        out = jnp.where(lanes_of == j, values[j], out)
    return out


def shifts():
    return [(ox, oy) for ox in (-1, 0, 1) for oy in (-1, 0, 1)]


def inside(shape, ox, oy):
    lanes = iota(shape, 1)
    x = lanes // 4 % 4 + ox
    y = lanes % 4 + oy
    return (x >= 0) & (x < 4) & (y >= 0) & (y < 4)


def rolled(x, ox, oy):
    if ox == 0 and oy == 0:
        return x
    moved = pltpu.roll(x, (-(4 * ox + oy)) % 128, 1)
    return jnp.where(inside(x.shape, ox, oy), moved, 0.0)


def box(x):
    rows = iota(x.shape, 0) % 4
    lanes = iota(x.shape, 1)
    count = x.shape[0]
    x = (
        x
        + jnp.where(rows > 0, pltpu.roll(x, 1, 0), 0.0)
        + jnp.where(rows < 3, pltpu.roll(x, count - 1, 0), 0.0)
    )
    for step, place in ((1, lanes % 4), (4, lanes // 4 % 4)):
        x = (
            x
            + jnp.where(place > 0, pltpu.roll(x, step, 1), 0.0)
            + jnp.where(place < 3, pltpu.roll(x, 128 - step, 1), 0.0)
        )
    return x / 27.0


def cat_rows(x):
    return jnp.concatenate([x[:, 128 * z : 128 * z + 128] for z in range(4)], axis=0)


def dot(a, b, dims=None, precision=None):
    if dims is None:
        dims = (((1,), (0,)), ((), ()))
    return lax.dot_general(a, b, dims, precision=precision, preferred_element_type=F32)


def whole_kernel(
    fields_hbm, visc_hbm, samples, trainers, w1_hbm, w2_hbm, w3_hbm,
    adv_hbm, loss_out, first_out, second_out, third_out,
    start, mid, adv, y_send, y_recv, z_send, z_recv, y_send2, y_recv2, z_send2, z_recv2,
    halo_z, t_send, t_recv, l_send, l_recv, w1, w2, w3, st1, st2,
    grads, part, sum1, spread, sum2, final,
    local_sem, x_s, x_r, y_s, y_r, z_s, z_r, x2_s, x2_r, y2_s, y2_r, z2_s, z2_r,
    t_s, t_r, l_s, l_r, a_s, a_r, b_s, b_r, c_s, c_r,
):
    ax = lax.axis_index("gx")
    ay = lax.axis_index("gy")
    az = lax.axis_index("gz")
    aw = ax * NZ + az

    def in_y(d):
        return (ax, lax.rem(ay + d, NY), az)

    def in_w(d):
        w = lax.rem(aw + d, NX * NZ)
        return (w // NZ, ay, lax.rem(w, NZ))

    loads = [
        pltpu.make_async_copy(fields_hbm, start.at[0:4, 1:9], local_sem.at[0]),
        pltpu.make_async_copy(visc_hbm, start.at[4, 1:9], local_sem.at[1]),
        pltpu.make_async_copy(w1_hbm, w1, local_sem.at[2]),
        pltpu.make_async_copy(w2_hbm, w2, local_sem.at[3]),
        pltpu.make_async_copy(w3_hbm, w3, local_sem.at[4]),
    ]
    for load in loads:
        load.start()

    barrier = pltpu.get_barrier_semaphore()

    def greet(d, carry):
        pl.semaphore_signal(barrier, inc=1, device_id=in_y(d), device_id_type=MESH)
        pl.semaphore_signal(barrier, inc=1, device_id=in_w(d), device_id_type=MESH)
        return carry

    lax.fori_loop(1, 16, greet, 0)
    picked = [samples[j] for j in range(8)]
    owners = [trainers[j] for j in range(8)]
    t_send[...] = by_lane(owners, iota((1, 128), 1) % 8)
    loads[0].wait()
    loads[1].wait()
    pl.semaphore_wait(barrier, 30)

    def remote(src, dst, s, r, to):
        return pltpu.make_async_remote_copy(
            src_ref=src, dst_ref=dst, send_sem=s, recv_sem=r, device_id=to, device_id_type=MESH
        )

    x_up = (lax.rem(ax + 1, NX), ay, az)
    x_down = (lax.rem(ax + NX - 1, NX), ay, az)
    other = (ax, ay, 1 - az)

    def exchange_x(ref, s, r):
        return [
            remote(ref.at[:, 8], ref.at[:, 0], s.at[0], r.at[0], x_up),
            remote(ref.at[:, 1], ref.at[:, 9], s.at[1], r.at[1], x_down),
        ]

    def exchange_yz(ys, yr, zs, zr, ysem, yrem, zsem, zrem):
        return [
            remote(ys.at[1], yr.at[0], ysem.at[0], yrem.at[0], in_y(1)),
            remote(ys.at[0], yr.at[1], ysem.at[1], yrem.at[1], in_y(NY - 1)),
            remote(zs, zr, zsem, zrem, other),
        ]

    moves = exchange_x(start, x_s, x_r)
    for move in moves:
        move.start()
    pack_sides(start, 5, y_send, z_send)
    sides = exchange_yz(y_send, y_recv, z_send, z_recv, y_s, y_r, z_s, z_r)
    for move in sides:
        move.start()

    def everyone(src, buf, s, r, slot, to):
        def begin(d, carry):
            remote(src, buf.at[slot], s.at[d], r.at[slot], to(d)).start()
            return carry

        lax.fori_loop(1, 16, begin, 0)

    def all_here(src, buf, s, r, slot, to):
        def finish(d, carry):
            at = lax.rem(slot + d, 16)
            copy = remote(src, buf.at[at], s.at[d], r.at[at], to(d))
            copy.wait_send()
            copy.wait_recv()
            return carry

        lax.fori_loop(1, 16, finish, 0)

    everyone(t_send, t_recv, t_s, t_r, ay, in_y)
    t_recv[ay] = t_send[...]

    for move in sides:
        move.wait()
    unpack_sides(z_recv, 5, halo_z)
    for move in moves:
        move.wait()

    def visc(p):
        return start[4, p]

    def store_mid(p):
        for c, x in enumerate(advance_plane(start, visc, y_recv, y_recv, halo_z, p)):
            mid[c, p] = x

    store_mid(1)
    store_mid(8)
    moves = exchange_x(mid, x2_s, x2_r)
    for move in moves:
        move.start()

    def first_step(p, carry):
        store_mid(p)
        return carry

    lax.fori_loop(2, 8, first_step, 0)
    pack_sides(mid, 4, y_send2, z_send2)
    sides = exchange_yz(y_send2, y_recv2, z_send2, z_recv2, y2_s, y2_r, z2_s, z2_r)
    for move in sides:
        move.start()
    for move in sides:
        move.wait()
    unpack_sides(z_recv2, 4, halo_z)

    def store_adv(p):
        for c, x in enumerate(advance_plane(mid, visc, y_recv2, y_recv, halo_z, p)):
            adv[c, p - 1] = x

    def second_step(p, carry):
        store_adv(p)
        return carry

    lax.fori_loop(2, 8, second_step, 0)
    for move in moves:
        move.wait()
    store_adv(1)
    store_adv(8)
    write = pltpu.make_async_copy(adv, adv_hbm, local_sem.at[5])
    write.start()

    row = iota((128, 256), 0)
    base = by_lane([(s // 256) * 128 + (s // 32 % 8) * 4 for s in picked], row // 16)
    want = base + row // 4 % 4 * 32 + row % 4
    hot = jnp.where(want == iota((128, 256), 1), 1.0, 0.0).astype(BF16)
    lanes128 = iota((128, 128), 1)
    keep = by_lane([s % 32 for s in picked], iota((128, 128), 0) // 16) == lanes128 // 4
    frow = iota((64, 128), 0)
    flane = iota((64, 128), 1)
    comp = frow % 4
    zrow = frow // 4
    for i, c in enumerate(PAIR_P + PAIR_Q):
        here = (frow >= 16 + 4 * i) & (frow < 20 + 4 * i)
        comp = jnp.where(here, c, comp)
    zrow = jnp.where(frow < 16, zrow, frow % 4)
    cells = jnp.zeros((64, 128), F32)
    for c in range(4):
        plane = adv[c].reshape(256, 128).astype(BF16)
        found = jnp.where(keep, dot(hot, plane), 0.0).astype(BF16)
        fold = jnp.where((comp == c) & (flane % 4 == zrow), 1.0, 0.0).astype(BF16)
        cells = cells + dot(fold, found, NT)

    loads[2].wait()
    loads[3].wait()
    loads[4].wait()
    st1[...] = jnp.zeros_like(st1)
    chosen = cells[0:16]
    for i, (ox, oy) in enumerate(shifts()):
        moved = rolled(chosen, ox, oy)
        for o in range(3):
            k = 3 * i + o
            for z in range(4):
                if 0 <= z + o - 1 < 4:
                    st1[4 * k : 4 * k + 4, 128 * z : 128 * z + 128] = moved[
                        4 * (z + o - 1) : 4 * (z + o - 1) + 4
                    ]
    pre1 = cat_rows(dot(w1[...], st1[0:108, :].astype(BF16)))
    sig1 = jax.nn.sigmoid(pre1)
    slope1 = sig1 * (1.0 + pre1 * (1.0 - sig1))
    hid1 = (pre1 * sig1).astype(BF16).astype(F32)
    for i, (ox, oy) in enumerate(shifts()):
        moved = rolled(hid1, ox, oy).astype(BF16)
        for o in range(3):
            k = 3 * i + o
            for z in range(4):
                if 0 <= z + o - 1 < 4:
                    piece = moved[32 * (z + o - 1) : 32 * (z + o)]
                else:
                    piece = jnp.zeros((32, 128), BF16)
                st2[32 * k : 32 * k + 32, 128 * z : 128 * z + 128] = piece
    pre2 = cat_rows(dot(w2[...], st2[0:864, :]))
    sig2 = jax.nn.sigmoid(pre2)
    slope2 = sig2 * (1.0 + pre2 * (1.0 - sig2))
    hid2 = (pre2 * sig2).astype(BF16)
    pick_row = jnp.where(iota((24, 6), 0) // 4 == iota((24, 6), 1), 1.0, 0.0).astype(BF16)
    pick_col = jnp.where(iota((32, 128), 1) % 32 == iota((32, 128), 0), 1.0, 0.0).astype(BF16)
    spread3 = dot(dot(pick_row, w3[...]).astype(BF16), pick_col)
    same_z = iota((24, 128), 0) % 4 == iota((24, 128), 1) // 32
    wide3 = jnp.where(same_z, spread3, 0.0).astype(BF16)
    predicted = dot(wide3, hid2)
    up_p, up_q = cells[16:40], cells[40:64]
    target = box(up_p * up_q) - box(up_p) * box(up_q)
    misfit = predicted - target

    squares = jnp.broadcast_to(jnp.sum(misfit * misfit, axis=0, keepdims=True), (8, 128))
    group = jnp.where(iota((128, 128), 0) // 16 == lanes128 % 8, 1.0, 0.0)
    l_send[...] = dot(squares, group, precision=HIGH)[0:1] / 384.0
    all_here(t_send, t_recv, t_s, t_r, ay, in_y)
    everyone(l_send, l_recv, l_s, l_r, ay, in_y)
    l_recv[ay] = l_send[...]
    owned = t_recv[:, 0, :]
    mine = by_lane(owners, iota((16, 128), 1) // 16)
    load = jnp.zeros((16, 128), F32)
    for s in range(8):
        other_owner = owned if s == 0 else pltpu.roll(owned, s, 1)
        load = load + jnp.where(other_owner == mine, 1.0, 0.0)
    load = jnp.sum(load, axis=0, keepdims=True)
    share = 1.0 / (WORKERS * jnp.maximum(load, 1.0))
    grad_pred = (misfit * (share * (2.0 / 384.0))).astype(BF16)

    third = jnp.where(same_z, dot(grad_pred, hid2, NT), 0.0)
    third = jnp.concatenate(
        [jnp.sum(third[4 * i : 4 * i + 4], axis=0, keepdims=True) for i in range(6)]
        + [jnp.zeros((26, 128), F32)],
        axis=0,
    )
    third = third + pltpu.roll(third, 32, 1)
    third = third + pltpu.roll(third, 64, 1)
    grad_mid = (dot(wide3, grad_pred, TN) * slope2).astype(BF16)
    mid_cols = jnp.concatenate([grad_mid[32 * z : 32 * z + 32] for z in range(4)], axis=1)

    def send_tile(i):
        for h in range(2):
            to = 2 * i + h

            @pl.when(ay != to)
            def _():
                remote(grads.at[to], part.at[ay], a_s.at[to], a_r.at[ay], (ax, to, az)).start()

    def store_tile(i, x):
        grads[2 * i] = x[0:16]
        grads[2 * i + 1] = x[16:32]

    for i in range(7):
        rows_here = 128 if i < 6 else 96
        tile = dot(mid_cols, st2[128 * i : 128 * i + rows_here, :], NT)
        if i == 6:
            tile = jnp.concatenate([tile, third[:, 96:128]], axis=1)
        store_tile(i, tile)
        send_tile(i)
    lower = jnp.zeros((128, 128), F32)
    for i, (ox, oy) in enumerate(shifts()):
        y = dot(w2[:, 96 * i : 96 * i + 96], mid_cols, TN)
        parts = []
        for z in range(4):
            total = y[32:64, 128 * z : 128 * z + 128]
            if z + 1 < 4:
                total = total + y[0:32, 128 * z + 128 : 128 * z + 256]
            if z - 1 >= 0:
                total = total + y[64:96, 128 * z - 128 : 128 * z]
            parts.append(total)
        lower = lower + rolled(jnp.concatenate(parts, axis=0), -ox, -oy)
    entry = (lower * slope1).astype(BF16)
    entry_cols = jnp.concatenate([entry[32 * z : 32 * z + 32] for z in range(4)], axis=1)
    store_tile(7, dot(entry_cols, st1[...].astype(BF16), NT))
    send_tile(7)

    part[ay] = grads[ay]
    for to in range(16):

        @pl.when(ay != to)
        def _():
            remote(grads.at[to], part.at[to], a_s.at[to], a_r.at[to], (ax, to, az)).wait()

    def added(buf):
        total = buf[0]
        for s in range(1, 16):
            total = total + buf[s]
        return total

    sum1[...] = added(part)
    everyone(sum1, spread, b_s, b_r, aw, in_w)
    spread[aw] = sum1[...]
    all_here(sum1, spread, b_s, b_r, aw, in_w)
    sum2[...] = added(spread)
    everyone(sum2, final, c_s, c_r, ay, in_y)
    final[ay] = sum2[...]

    all_here(l_send, l_recv, l_s, l_r, ay, in_y)
    lanes16 = iota((16, 128), 1)
    rank = jnp.zeros((16, 128), I32)
    for s in range(1, 8):
        earlier = (pltpu.roll(owned, s, 1) == owned) & (lanes16 % 8 >= s)
        rank = rank + jnp.where(earlier, 1, 0)
    losses = l_recv[:, 0, :]
    own = (owned == ay) & (lanes16 < 8)
    place = lanes16 - 2 * iota((16, 128), 0)
    slots = jnp.zeros((16, 128), F32)
    for r in range(2):
        value = jnp.sum(jnp.where(own & (rank == r), losses, 0.0), axis=1, keepdims=True)
        slots = slots + jnp.where(place == r, value, 0.0)
    loss_out[...] = jnp.sum(slots, axis=0, keepdims=True)[:, 0:32]

    all_here(sum2, final, c_s, c_r, ay, in_y)
    for i in range(6):
        second_out[:, 128 * i : 128 * i + 128] = final[2 * i : 2 * i + 2].reshape(32, 128)
    last = final[12:14].reshape(32, 128)
    second_out[:, 768:864] = last[:, 0:96]
    third_out[...] = last[0:6, 96:128]
    first_out[...] = final[14:16].reshape(32, 128)[:, 0:108]
    write.wait()


def on_device(fields, viscosity, samples, trainers, conv_first, conv_second, conv_third):
    vmem = pl.BlockSpec(memory_space=pltpu.VMEM)
    smem = pl.BlockSpec(memory_space=pltpu.SMEM)
    hbm = pl.BlockSpec(memory_space=pl.ANY)
    dma = pltpu.SemaphoreType.DMA
    v = pltpu.VMEM
    advanced, losses, first, second, third = pl.pallas_call(
        whole_kernel,
        out_shape=(
            jax.ShapeDtypeStruct((4, 8, 32, 128), F32),
            jax.ShapeDtypeStruct((1, 32), F32),
            jax.ShapeDtypeStruct((32, 108), F32),
            jax.ShapeDtypeStruct((32, 864), F32),
            jax.ShapeDtypeStruct((6, 32), F32),
        ),
        in_specs=[hbm, hbm, smem, smem, hbm, hbm, hbm],
        out_specs=(hbm, vmem, vmem, vmem, vmem),
        scratch_shapes=[
            v((5, 10, 32, 128), F32), v((4, 10, 32, 128), F32), v((4, 8, 32, 128), F32),
            v((2, 5, 8, 128), F32), v((2, 5, 8, 128), F32),
            v((2, 16, 128), F32), v((2, 16, 128), F32),
            v((2, 4, 8, 128), F32), v((2, 4, 8, 128), F32),
            v((2, 8, 128), F32), v((2, 8, 128), F32),
            v((5, 8, 32, 128), F32),
            v((1, 128), I32), v((16, 1, 128), I32), v((1, 128), F32), v((16, 1, 128), F32),
            v((32, 108), BF16), v((32, 864), BF16), v((6, 32), BF16),
            v((128, 512), F32), v((864, 512), BF16),
            v((16, 16, 128), F32), v((16, 16, 128), F32), v((16, 128), F32),
            v((16, 16, 128), F32), v((16, 128), F32), v((16, 16, 128), F32),
            dma((6,)),
            dma((2,)), dma((2,)), dma((2,)), dma((2,)), dma, dma,
            dma((2,)), dma((2,)), dma((2,)), dma((2,)), dma, dma,
            dma((16,)), dma((16,)), dma((16,)), dma((16,)),
            dma((16,)), dma((16,)), dma((16,)), dma((16,)), dma((16,)), dma((16,)),
        ],
        compiler_params=pltpu.CompilerParams(
            collective_id=0, has_side_effects=True, vmem_limit_bytes=48 * 1024 * 1024
        ),
        name="step",
    )(
        fields, viscosity, samples.reshape(8), trainers.reshape(8),
        conv_first, conv_second, conv_third,
    )
    return advanced, losses.reshape(1, 1, 1, 32), first, second, third


def solution(mesh):
    in_specs = (
        P(None, "gx", "gy", "gz"),
        P("gx", "gy", "gz"),
        P("gx", "gy", "gz", None),
        P("gx", "gy", "gz", None, None),
        P(),
        P(),
        P(),
    )
    out_specs = (P(None, "gx", "gy", "gz"), P("gx", "gy", "gz", None), P(), P(), P())
    return jax.shard_map(
        on_device, mesh=mesh, in_specs=in_specs, out_specs=out_specs, check_vma=False
    )
```

profile of v0, /device:TPU:1, one launch (start us, length us, event | category | flops | bytes accessed | tf_op | source)
XLA Modules:
  0.0 54.9 jit_solution(15756988257597177876)
XLA Ops:
  0.6 0.0 copy-start.4
  0.6 0.0 copy-start.5
  0.7 0.0 copy-start.6
  0.7 0.7 %copy-done.4 = bf16[6,32]{1,0:T(8,128)(2,1)S(1)} copy-done((bf16[6,32]{1,0:T(8,128)(2,1)S(1)}, bf16[6,32]{1,0:T(8,128)(2,1)}, u32[]{:S(2)}) %copy-start.4) | copy-done | bytes 408
  1.3 0.0 copy-done.5
  1.3 0.0 copy-done.6
  1.3 0.0 copy-start
  1.3 1.0 %copy-done = f32[4,8,32,128]{3,2,1,0:T(8,128)S(1)} copy-done((f32[4,8,32,128]{3,2,1,0:T(8,128)S(1)}, f32[4,8,32,128]{3,2,1,0:T(8,128)}, u32[]{:S(2)}) %copy-start) | copy-done | bytes 524312
  2.4 0.0 copy-start.1
  2.4 0.9 %copy-done.1 = f32[8,32,128]{2,1,0:T(8,128)S(1)} copy-done((f32[8,32,128]{2,1,0:T(8,128)S(1)}, f32[8,32,128]{2,1,0:T(8,128)}, u32[]{:S(2)}) %copy-start.1) | copy-done | bytes 131096
  3.3 0.0 copy-start.2
  3.3 0.8 %copy-done.2 = bf16[32,864]{1,0:T(8,128)(2,1)S(1)} copy-done((bf16[32,864]{1,0:T(8,128)(2,1)S(1)}, bf16[32,864]{1,0:T(8,128)(2,1)}, u32[]{:S(2)}) %copy-start.2) | copy-done | bytes 55320
  4.1 0.0 copy-start.3
  4.1 0.7 %copy-done.3 = bf16[32,108]{1,0:T(8,128)(2,1)S(1)} copy-done((bf16[32,108]{1,0:T(8,128)(2,1)S(1)}, bf16[32,108]{1,0:T(8,128)(2,1)}, u32[]{:S(2)}) %copy-start.3) | copy-done | bytes 6936
  4.8 47.0 %step.1 = (f32[4,8,32,128]{3,2,1,0:T(8,128)S(1)}, f32[1,32]{1,0:T(1,128)S(1)}, f32[32,108]{1,0:T(8,128)S(1)}, f32[32,864]{1,0:T(8,128)S(1)}, f32[6,32]{1,0:T(8,128)S(1)}) custom-call(f32[4,8,32,128]{3,2,1,0:T(8,128)S(1)} %copy-done, f32[8,32,128]{2,1,0:T(8,128)S(1)} %copy-done.1, s32[8]{0:T(128)S(1)} %bitcast.3, s32[8]{0:T(128)S(1)} %bitcast.4, ...), custom_call_target="tpu_custom_call" | custom-call | tf_op jit(solution)/shard_map/step/pallas_call | solution.py:474
  51.8 0.8 %copy.17 = f32[4,8,32,128]{3,2,1,0:T(8,128)} copy(f32[4,8,32,128]{3,2,1,0:T(8,128)S(1)} %get-tuple-element.20) | data formatting | bytes 1048576
  52.6 0.5 copy.18
  53.1 0.6 %copy.19 = f32[32,108]{1,0:T(8,128)} copy(f32[32,108]{1,0:T(8,128)S(1)} %get-tuple-element.22) | data formatting | bytes 27648
  53.7 0.6 %copy.20 = f32[32,864]{1,0:T(8,128)} copy(f32[32,864]{1,0:T(8,128)S(1)} %get-tuple-element.23) | data formatting | bytes 221184
  54.4 0.6 %copy.21 = f32[6,32]{1,0:T(8,128)} copy(f32[6,32]{1,0:T(8,128)S(1)} %get-tuple-element.24) | data formatting | bytes 1536
Async XLA Ops:
  0.6 0.7 %copy-start.4 = (bf16[6,32]{1,0:T(8,128)(2,1)S(1)}, bf16[6,32]{1,0:T(8,128)(2,1)}, u32[]{:S(2)}) copy-start(bf16[6,32]{1,0:T(8,128)(2,1)} %w3_hbm.1) | copy-start | bytes 1156
  0.6 0.7 %copy-start.5 = (s32[1,1,1,8]{3,2,1,0:T(1,128)S(1)}, s32[1,1,1,8]{3,2,1,0:T(1,128)}, u32[]{:S(2)}) copy-start(s32[1,1,1,8]{3,2,1,0:T(1,128)} %param.9) | copy-start | bytes 100
  0.7 0.7 %copy-start.6 = (s32[1,1,1,8,1]{3,4,2,1,0:T(1,128)S(1)}, s32[1,1,1,8,1]{3,4,2,1,0:T(1,128)}, u32[]{:S(2)}) copy-start(s32[1,1,1,8,1]{3,4,2,1,0:T(1,128)} %param.10) | copy-start | bytes 100
  1.3 1.0 %copy-start = (f32[4,8,32,128]{3,2,1,0:T(8,128)S(1)}, f32[4,8,32,128]{3,2,1,0:T(8,128)}, u32[]{:S(2)}) copy-start(f32[4,8,32,128]{3,2,1,0:T(8,128)} %fields_hbm.1) | copy-start | bytes 1572868
  2.4 0.9 %copy-start.1 = (f32[8,32,128]{2,1,0:T(8,128)S(1)}, f32[8,32,128]{2,1,0:T(8,128)}, u32[]{:S(2)}) copy-start(f32[8,32,128]{2,1,0:T(8,128)} %visc_hbm.1) | copy-start | bytes 393220
  3.3 0.8 %copy-start.2 = (bf16[32,864]{1,0:T(8,128)(2,1)S(1)}, bf16[32,864]{1,0:T(8,128)(2,1)}, u32[]{:S(2)}) copy-start(bf16[32,864]{1,0:T(8,128)(2,1)} %w2_hbm.1) | copy-start | bytes 165892
  4.1 0.7 %copy-start.3 = (bf16[32,108]{1,0:T(8,128)(2,1)S(1)}, bf16[32,108]{1,0:T(8,128)(2,1)}, u32[]{:S(2)}) copy-start(bf16[32,108]{1,0:T(8,128)(2,1)} %w1_hbm.1) | copy-start | bytes 20740
where the time goes:
time: 55.2 us; the launch traced here: 54.9 us
  Pallas kernels  47 us (85%)
  local copies, waits for them, and re-layouts  7.27 us (13%)
  between operations  0.67 us (1%)
    pallas_call x1, Pallas kernels, on_device(): pl.pallas_call(whole_kernel, out_shape=(jax.ShapeDtypeStruct((4, 8, 32, 1...  47 us
    unnamed x19, local copies, waits for them, and re-layouts  7.27 us

commit v1 on v0

--- a/solution.py
+++ b/solution.py
@@ -151,10 +151,10 @@
 
 def whole_kernel(
     fields_hbm, visc_hbm, samples, trainers, w1_hbm, w2_hbm, w3_hbm,
-    adv_hbm, loss_out, first_out, second_out, third_out,
+    adv_hbm, loss_hbm, final,
     start, mid, adv, y_send, y_recv, z_send, z_recv, y_send2, y_recv2, z_send2, z_recv2,
     halo_z, t_send, t_recv, l_send, l_recv, w1, w2, w3, st1, st2,
-    grads, part, sum1, spread, sum2, final,
+    grads, part, sum1, spread, sum2, loss_out,
     local_sem, x_s, x_r, y_s, y_r, z_s, z_r, x2_s, x2_r, y2_s, y2_r, z2_s, z2_r,
     t_s, t_r, l_s, l_r, a_s, a_r, b_s, b_r, c_s, c_r,
 ):
@@ -387,9 +387,11 @@
         for h in range(2):
             to = 2 * i + h
 
-            @pl.when(ay != to)
+            @pl.when(aw != to)
             def _():
-                remote(grads.at[to], part.at[ay], a_s.at[to], a_r.at[ay], (ax, to, az)).start()
+                remote(
+                    grads.at[to], part.at[aw], a_s.at[to], a_r.at[aw], (to // NZ, ay, to % NZ)
+                ).start()
 
     def store_tile(i, x):
         grads[2 * i] = x[0:16]
@@ -419,12 +421,14 @@
     store_tile(7, dot(entry_cols, st1[...].astype(BF16), NT))
     send_tile(7)
 
-    part[ay] = grads[ay]
+    part[aw] = grads[aw]
     for to in range(16):
 
-        @pl.when(ay != to)
+        @pl.when(aw != to)
         def _():
-            remote(grads.at[to], part.at[to], a_s.at[to], a_r.at[to], (ax, to, az)).wait()
+            remote(
+                grads.at[to], part.at[to], a_s.at[to], a_r.at[to], (to // NZ, ay, to % NZ)
+            ).wait()
 
     def added(buf):
         total = buf[0]
@@ -433,12 +437,8 @@
         return total
 
     sum1[...] = added(part)
-    everyone(sum1, spread, b_s, b_r, aw, in_w)
-    spread[aw] = sum1[...]
-    all_here(sum1, spread, b_s, b_r, aw, in_w)
-    sum2[...] = added(spread)
-    everyone(sum2, final, c_s, c_r, ay, in_y)
-    final[ay] = sum2[...]
+    everyone(sum1, spread, b_s, b_r, ay, in_y)
+    spread[ay] = sum1[...]
 
     all_here(l_send, l_recv, l_s, l_r, ay, in_y)
     lanes16 = iota((16, 128), 1)
@@ -454,34 +454,72 @@
         value = jnp.sum(jnp.where(own & (rank == r), losses, 0.0), axis=1, keepdims=True)
         slots = slots + jnp.where(place == r, value, 0.0)
     loss_out[...] = jnp.sum(slots, axis=0, keepdims=True)[:, 0:32]
-
-    all_here(sum2, final, c_s, c_r, ay, in_y)
+    write_loss = pltpu.make_async_copy(loss_out, loss_hbm, local_sem.at[6])
+    write_loss.start()
+
+    all_here(sum1, spread, b_s, b_r, ay, in_y)
+    sum2[...] = added(spread)
+    everyone(sum2, final, c_s, c_r, aw, in_w)
+    own_part = pltpu.make_async_copy(sum2, final.at[aw], local_sem.at[7])
+    own_part.start()
+    write.wait()
+    write_loss.wait()
+    own_part.wait()
+    all_here(sum2, final, c_s, c_r, aw, in_w)
+
+
+def hand_over_kernel(
+    adv_in, loss_in, final_in, adv_out, loss_out, first_out, second_out, third_out,
+    adv, loss, final, first, second, third, sem,
+):
+    loads = [pltpu.make_async_copy(adv_in.at[c], adv.at[c], sem.at[c]) for c in range(4)]
+    loads.append(pltpu.make_async_copy(loss_in, loss, sem.at[4]))
+    load_final = pltpu.make_async_copy(final_in, final, sem.at[5])
+    load_final.start()
+    for load in loads:
+        load.start()
+    load_final.wait()
     for i in range(6):
-        second_out[:, 128 * i : 128 * i + 128] = final[2 * i : 2 * i + 2].reshape(32, 128)
+        second[:, 128 * i : 128 * i + 128] = final[2 * i : 2 * i + 2].reshape(32, 128)
     last = final[12:14].reshape(32, 128)
-    second_out[:, 768:864] = last[:, 0:96]
-    third_out[...] = last[0:6, 96:128]
-    first_out[...] = final[14:16].reshape(32, 128)[:, 0:108]
-    write.wait()
+    second[:, 768:864] = last[:, 0:96]
+    third[...] = last[0:6, 96:128]
+    first[...] = final[14:16].reshape(32, 128)[:, 0:108]
+    stores = [
+        pltpu.make_async_copy(second, second_out, sem.at[6]),
+        pltpu.make_async_copy(first, first_out, sem.at[7]),
+        pltpu.make_async_copy(third, third_out, sem.at[8]),
+    ]
+    for store in stores:
+        store.start()
+    for c in range(4):
+        loads[c].wait()
+        stores.append(pltpu.make_async_copy(adv.at[c], adv_out.at[c], sem.at[9 + c]))
+        stores[-1].start()
+    loads[4].wait()
+    stores.append(pltpu.make_async_copy(loss, loss_out, sem.at[13]))
+    stores[-1].start()
+    for store in stores:
+        store.wait()
 
 
 def on_device(fields, viscosity, samples, trainers, conv_first, conv_second, conv_third):
-    vmem = pl.BlockSpec(memory_space=pltpu.VMEM)
     smem = pl.BlockSpec(memory_space=pltpu.SMEM)
     hbm = pl.BlockSpec(memory_space=pl.ANY)
     dma = pltpu.SemaphoreType.DMA
     v = pltpu.VMEM
-    advanced, losses, first, second, third = pl.pallas_call(
+    shapes = (
+        jax.ShapeDtypeStruct((4, 8, 32, 128), F32),
+        jax.ShapeDtypeStruct((1, 32), F32),
+        jax.ShapeDtypeStruct((32, 108), F32),
+        jax.ShapeDtypeStruct((32, 864), F32),
+        jax.ShapeDtypeStruct((6, 32), F32),
+    )
+    results = pl.pallas_call(
         whole_kernel,
-        out_shape=(
-            jax.ShapeDtypeStruct((4, 8, 32, 128), F32),
-            jax.ShapeDtypeStruct((1, 32), F32),
-            jax.ShapeDtypeStruct((32, 108), F32),
-            jax.ShapeDtypeStruct((32, 864), F32),
-            jax.ShapeDtypeStruct((6, 32), F32),
-        ),
+        out_shape=(shapes[0], shapes[1], jax.ShapeDtypeStruct((16, 16, 128), F32)),
         in_specs=[hbm, hbm, smem, smem, hbm, hbm, hbm],
-        out_specs=(hbm, vmem, vmem, vmem, vmem),
+        out_specs=(hbm,) * 3,
         scratch_shapes=[
             v((5, 10, 32, 128), F32), v((4, 10, 32, 128), F32), v((4, 8, 32, 128), F32),
             v((2, 5, 8, 128), F32), v((2, 5, 8, 128), F32),
@@ -493,21 +531,33 @@
             v((32, 108), BF16), v((32, 864), BF16), v((6, 32), BF16),
             v((128, 512), F32), v((864, 512), BF16),
             v((16, 16, 128), F32), v((16, 16, 128), F32), v((16, 128), F32),
-            v((16, 16, 128), F32), v((16, 128), F32), v((16, 16, 128), F32),
-            dma((6,)),
+            v((16, 16, 128), F32), v((16, 128), F32), v((1, 32), F32),
+            dma((8,)),
             dma((2,)), dma((2,)), dma((2,)), dma((2,)), dma, dma,
             dma((2,)), dma((2,)), dma((2,)), dma((2,)), dma, dma,
             dma((16,)), dma((16,)), dma((16,)), dma((16,)),
             dma((16,)), dma((16,)), dma((16,)), dma((16,)), dma((16,)), dma((16,)),
         ],
         compiler_params=pltpu.CompilerParams(
-            collective_id=0, has_side_effects=True, vmem_limit_bytes=48 * 1024 * 1024
+            collective_id=0, has_side_effects=True, vmem_limit_bytes=60 * 1024 * 1024
         ),
         name="step",
     )(
         fields, viscosity, samples.reshape(8), trainers.reshape(8),
         conv_first, conv_second, conv_third,
     )
+    advanced, losses, first, second, third = pl.pallas_call(
+        hand_over_kernel,
+        out_shape=shapes,
+        in_specs=[hbm] * 3,
+        out_specs=(hbm,) * 5,
+        scratch_shapes=[
+            v((4, 8, 32, 128), F32), v((1, 32), F32), v((16, 16, 128), F32),
+            v((32, 108), F32), v((32, 864), F32), v((6, 32), F32), dma((14,)),
+        ],
+        compiler_params=pltpu.CompilerParams(vmem_limit_bytes=60 * 1024 * 1024),
+        name="hand_over",
+    )(*results)
     return advanced, losses.reshape(1, 1, 1, 32), first, second, third
 
 

time: 55.2 us -> 45.3 us (0.82)
  local copies, waits for them, and re-layouts: 7.27 us -> 0 us
  Pallas kernels: 47 us -> 44.5 us
    unnamed x19 -> x0, local copies, waits for them, and re-layouts: 7.27 us -> none
    pallas_call x1 -> x2, Pallas kernels: 47 us -> 44.5 us  [the longest x1 42.6 us: on_device(): pl.pallas_call(whole_kernel, out_shape=(shapes[0], shapes[1], jax.ShapeDt...]
where the time goes in v1:
time: 45.3 us; the launch traced here: 45.1 us
  Pallas kernels  44.5 us (98%)
  between operations  0.64 us (1%)
    pallas_call x1, Pallas kernels, on_device(): pl.pallas_call(whole_kernel, out_shape=(shapes[0], shapes[1], jax.ShapeDt...  42.6 us
    pallas_call x1, Pallas kernels, on_device(): pl.pallas_call(hand_over_kernel, out_shape=shapes, in_specs=[hbm] * 3, ou...  1.94 us

profile of v1, /device:TPU:1, one launch (start us, length us, event | category | flops | bytes accessed | tf_op | source)
XLA Modules:
  0.0 45.1 jit_solution(202963245295428504)
XLA Ops:
  0.6 42.6 %step.1 = (f32[4,8,32,128]{3,2,1,0:T(8,128)}, f32[1,32]{1,0:T(1,128)}, f32[16,16,128]{2,1,0:T(8,128)}) custom-call(f32[4,8,32,128]{3,2,1,0:T(8,128)} %fields_hbm.1, f32[8,32,128]{2,1,0:T(8,128)} %visc_hbm.1, s32[8]{0:T(128)} %bitcast.3, s32[8]{0:T(128)} %bitcast.4, bf16[32,108]{1,0:T(8,128)(2,1)} %w1_hbm.1, bf16[32,864]{1,0:T(8,128)(2,1)} %w2_hbm.1, ...), custom_call_target="tpu_custom_call" | custom-call | tf_op jit(solution)/shard_map/step/pallas_call | solution.py:518
  43.2 1.9 %hand_over.1 = (f32[4,8,32,128]{3,2,1,0:T(8,128)}, f32[1,32]{1,0:T(1,128)}, f32[32,108]{1,0:T(8,128)}, f32[32,864]{1,0:T(8,128)}, f32[6,32]{1,0:T(8,128)}) custom-call(f32[4,8,32,128]{3,2,1,0:T(8,128)} %get-tuple-element.13.adv_in, f32[1,32]{1,0:T(1,128)} %get-tuple-element.14.loss_in, f32[16,16,128]{2,1,0:T(8,128)} %get-tuple-element.15.final_in), custom_call_target="tpu_custom_call" | custom-call | tf_op jit(solution)/shard_map/hand_over/pallas_call | solution.py:549

commit v2 on v1

--- a/solution.py
+++ b/solution.py
@@ -31,47 +31,74 @@
     return [speed * (a + b) - visc * (b - a) for a, b in zip(low, high)]
 
 
-def advance_plane(src, visc, halo_y, visc_y, halo_z, p):
+def inner_part(src, visc, store):
     rows = iota((32, 128), 0)
     lanes = iota((32, 128), 1)
-    q = [src[c, p] for c in range(4)]
-    v = visc(p)
-    q_before = [src[c, p - 1] for c in range(4)]
-    q_after = [src[c, p + 1] for c in range(4)]
-    total = [
-        a - b
-        for a, b in zip(flux(q, q_after, v, visc(p + 1), 0), flux(q_before, q, visc(p - 1), v, 0))
-    ]
-    at = pl.ds(p - 1, 1)
-    y_low = [halo_y[0, c, at] for c in range(4)]
-    y_high = [halo_y[1, c, at] for c in range(4)]
-
-    def up(x, edge):
-        return jnp.where(rows == 31, edge, pltpu.roll(x, 31, 0))
-
-    q_next = [up(x, e) for x, e in zip(q, y_high)]
-    faces = flux(q, q_next, v, up(v, visc_y[1, 4, at]), 1)
-    first = flux(y_low, [x[0:1] for x in q], visc_y[0, 4, at], v[0:1], 1)
-    total = [
-        t + (f - jnp.where(rows == 0, e, pltpu.roll(f, 1, 0)))
-        for t, f, e in zip(total, faces, first)
-    ]
-    side = [halo_z[c, p - 1] for c in range(4)]
-    side_v = halo_z[4, p - 1]
-
-    def along(x, edge):
-        return jnp.where(lanes == 127, edge, pltpu.roll(x, 127, 1))
-
-    q_next = [along(x, e) for x, e in zip(q, side)]
-    faces = flux(q, q_next, v, along(v, side_v), 2)
-    first = flux(side, q, side_v, v, 2)
-    total = [
-        t + (f - jnp.where(lanes == 0, e, pltpu.roll(f, 1, 1)))
-        for t, f, e in zip(total, faces, first)
-    ]
-    out = [x - TIME_STEP * t for x, t in zip(q, total)]
-    out[2] = out[2] + (TIME_STEP * BUOYANCY) * q[3]
-    return out
+
+    def plane(p, before, is_last):
+        q = [src[c, p] for c in range(4)]
+        v = visc(p)
+        if is_last:
+            after = None
+            total = [-b for b in before]
+        else:
+            after = flux(q, [src[c, p + 1] for c in range(4)], v, visc(p + 1), 0)
+            total = after if before is None else [a - b for a, b in zip(after, before)]
+        for axis, size, edge, d in ((0, 32, rows == 31, 1), (1, 128, lanes == 127, 2)):
+            q_next = [pltpu.roll(x, size - 1, axis) for x in q]
+            faces = flux(q, q_next, v, pltpu.roll(v, size - 1, axis), d)
+            faces = [jnp.where(edge, 0.0, f) for f in faces]
+            total = [t + (f - pltpu.roll(f, 1, axis)) for t, f in zip(total, faces)]
+        out = [x - TIME_STEP * t for x, t in zip(q, total)]
+        out[2] = out[2] + (TIME_STEP * BUOYANCY) * q[3]
+        store(p, out)
+        return after
+
+    def body(p, before):
+        return tuple(plane(p, before, False))
+
+    before = lax.fori_loop(2, 8, body, tuple(plane(1, None, False)))
+    plane(8, before, True)
+
+
+def edge_part(src, visc, dst, first, y_own, y_far, y_visc, z_own, z_far, z_visc):
+    rows = iota((128, 128), 0)
+    own_low = [z_own[0, 2 * c : 2 * c + 2] for c in range(4)]
+    own_high = [z_own[1, 2 * c : 2 * c + 2] for c in range(4)]
+    far_low = [z_far[0, 2 * c : 2 * c + 2] for c in range(4)]
+    far_high = [z_far[1, 2 * c : 2 * c + 2] for c in range(4)]
+    (v_own, v_far) = z_visc
+    low = flux(far_high, own_low, v_far[1, 8:10], v_own[0, 8:10], 2)
+    high = flux(own_high, far_low, v_own[1, 8:10], v_far[0, 8:10], 2)
+    for c in range(4):
+        for h in range(2):
+            placed = jnp.where(
+                rows == 0,
+                TIME_STEP * low[c][h : h + 1],
+                jnp.where(rows == 127, -TIME_STEP * high[c][h : h + 1], 0.0),
+            )
+            planes = slice(first + 4 * h, first + 4 * h + 4)
+            dst[c, planes] = dst[c, planes] + placed.T.reshape(4, 32, 128)
+    (v_own, v_far) = y_visc
+
+    def face(ref, side):
+        return [ref[side, c] for c in range(4)]
+
+    low = flux(face(y_far, 0), face(y_own, 0), v_far[0, 4], v_own[0, 4], 1)
+    high = flux(face(y_own, 1), face(y_far, 1), v_own[1, 4], v_far[1, 4], 1)
+    planes = slice(first, first + 8)
+    for c in range(4):
+        dst[c, planes, 0, :] = dst[c, planes, 0, :] + TIME_STEP * low[c]
+        dst[c, planes, 31, :] = dst[c, planes, 31, :] - TIME_STEP * high[c]
+
+    def of(p):
+        return [src[c, p] for c in range(4)]
+
+    low = flux(of(0), of(1), visc(0), visc(1), 0)
+    high = flux(of(8), of(9), visc(8), visc(9), 0)
+    for c in range(4):
+        dst[c, first] = dst[c, first] + TIME_STEP * low[c]
+        dst[c, first + 7] = dst[c, first + 7] - TIME_STEP * high[c]
 
 
 def pack_sides(src, count, y_send, z_send):
@@ -85,17 +112,6 @@
             z_send[1, g : g + 1, :] = turned[127:128]
 
 
-def unpack_sides(z_recv, count, halo_z):
-    rows = iota((128, 128), 0)
-    for c in range(count):
-        for h in range(2):
-            g = 2 * c + h
-            first = z_recv[0, g : g + 1, :]
-            last = z_recv[1, g : g + 1, :]
-            placed = jnp.where(rows == 0, last, jnp.where(rows == 127, first, 0.0))
-            halo_z[c, 4 * h : 4 * h + 4] = placed.T.reshape(4, 32, 128)
-
-
 def by_lane(values, lanes_of):
     out = jnp.zeros(lanes_of.shape, I32)
     for j in range(8):
@@ -107,18 +123,17 @@
     return [(ox, oy) for ox in (-1, 0, 1) for oy in (-1, 0, 1)]
 
 
-def inside(shape, ox, oy):
-    lanes = iota(shape, 1)
+def inside(ox, oy):
+    lanes = iota((1, 128), 1)
     x = lanes // 4 % 4 + ox
     y = lanes % 4 + oy
-    return (x >= 0) & (x < 4) & (y >= 0) & (y < 4)
+    return jnp.where((x >= 0) & (x < 4) & (y >= 0) & (y < 4), 1.0, 0.0)
 
 
 def rolled(x, ox, oy):
     if ox == 0 and oy == 0:
         return x
-    moved = pltpu.roll(x, (-(4 * ox + oy)) % 128, 1)
-    return jnp.where(inside(x.shape, ox, oy), moved, 0.0)
+    return pltpu.roll(x, (-(4 * ox + oy)) % 128, 1) * inside(ox, oy)
 
 
 def box(x):
@@ -150,10 +165,11 @@
 
 
 def whole_kernel(
-    fields_hbm, visc_hbm, samples, trainers, w1_hbm, w2_hbm, w3_hbm,
+    fields_hbm, visc_hbm, samples_hbm, trainers_hbm, w1_hbm, w2_hbm, w3_hbm,
     adv_hbm, loss_hbm, final,
+    samples, trainers,
     start, mid, adv, y_send, y_recv, z_send, z_recv, y_send2, y_recv2, z_send2, z_recv2,
-    halo_z, t_send, t_recv, l_send, l_recv, w1, w2, w3, st1, st2,
+    t_send, t_recv, l_send, l_recv, w1, w2, w3, w2_turned, hot, keep, folds, st1, st2,
     grads, part, sum1, spread, sum2, loss_out,
     local_sem, x_s, x_r, y_s, y_r, z_s, z_r, x2_s, x2_r, y2_s, y2_r, z2_s, z2_r,
     t_s, t_r, l_s, l_r, a_s, a_r, b_s, b_r, c_s, c_r,
@@ -171,15 +187,21 @@
         return (w // NZ, ay, lax.rem(w, NZ))
 
     loads = [
-        pltpu.make_async_copy(fields_hbm, start.at[0:4, 1:9], local_sem.at[0]),
-        pltpu.make_async_copy(visc_hbm, start.at[4, 1:9], local_sem.at[1]),
-        pltpu.make_async_copy(w1_hbm, w1, local_sem.at[2]),
-        pltpu.make_async_copy(w2_hbm, w2, local_sem.at[3]),
-        pltpu.make_async_copy(w3_hbm, w3, local_sem.at[4]),
+        pltpu.make_async_copy(src, dst, local_sem.at[i])
+        for i, (src, dst) in enumerate(
+            (
+                (fields_hbm, start.at[0:4, 1:9]),
+                (visc_hbm, start.at[4, 1:9]),
+                (trainers_hbm, trainers),
+                (samples_hbm, samples),
+                (w1_hbm, w1),
+                (w2_hbm, w2),
+                (w3_hbm, w3),
+            )
+        )
     ]
-    for load in loads:
-        load.start()
-
+    loads[0].start()
+    loads[1].start()
     barrier = pltpu.get_barrier_semaphore()
 
     def greet(d, carry):
@@ -188,11 +210,14 @@
         return carry
 
     lax.fori_loop(1, 16, greet, 0)
-    picked = [samples[j] for j in range(8)]
+    for load in loads[2:]:
+        load.start()
+    loads[0].wait()
+    loads[1].wait()
+    pack_sides(start, 5, y_send, z_send)
+    loads[2].wait()
     owners = [trainers[j] for j in range(8)]
     t_send[...] = by_lane(owners, iota((1, 128), 1) % 8)
-    loads[0].wait()
-    loads[1].wait()
     pl.semaphore_wait(barrier, 30)
 
     def remote(src, dst, s, r, to):
@@ -216,14 +241,6 @@
             remote(ys.at[0], yr.at[1], ysem.at[1], yrem.at[1], in_y(NY - 1)),
             remote(zs, zr, zsem, zrem, other),
         ]
-
-    moves = exchange_x(start, x_s, x_r)
-    for move in moves:
-        move.start()
-    pack_sides(start, 5, y_send, z_send)
-    sides = exchange_yz(y_send, y_recv, z_send, z_recv, y_s, y_r, z_s, z_r)
-    for move in sides:
-        move.start()
 
     def everyone(src, buf, s, r, slot, to):
         def begin(d, carry):
@@ -242,82 +259,97 @@
 
         lax.fori_loop(1, 16, finish, 0)
 
+    moves = exchange_x(start, x_s, x_r)
+    moves += exchange_yz(y_send, y_recv, z_send, z_recv, y_s, y_r, z_s, z_r)
+    for move in moves:
+        move.start()
     everyone(t_send, t_recv, t_s, t_r, ay, in_y)
     t_recv[ay] = t_send[...]
 
-    for move in sides:
-        move.wait()
-    unpack_sides(z_recv, 5, halo_z)
+    def visc(p):
+        return start[4, p]
+
+    def store_mid(p, out):
+        for c in range(4):
+            mid[c, p] = out[c]
+
+    inner_part(start, visc, store_mid)
+    loads[3].wait()
+    picked = [samples[j] for j in range(8)]
+    row = iota((128, 256), 0)
+    base = by_lane([(s // 256) * 128 + (s // 32 % 8) * 4 for s in picked], row // 16)
+    want = base + row // 4 % 4 * 32 + row % 4
+    hot[...] = jnp.where(want == iota((128, 256), 1), 1.0, 0.0).astype(BF16)
+    lanes128 = iota((128, 128), 1)
+    lz = by_lane([s % 32 for s in picked], iota((128, 128), 0) // 16)
+    keep[...] = jnp.where(lz == lanes128 // 4, 1.0, 0.0)
     for move in moves:
         move.wait()
-
-    def visc(p):
-        return start[4, p]
-
-    def store_mid(p):
-        for c, x in enumerate(advance_plane(start, visc, y_recv, y_recv, halo_z, p)):
-            mid[c, p] = x
-
-    store_mid(1)
-    store_mid(8)
+    edge_part(
+        start, visc, mid, 1, y_send, y_recv, (y_send, y_recv), z_send, z_recv, (z_send, z_recv)
+    )
+
     moves = exchange_x(mid, x2_s, x2_r)
     for move in moves:
         move.start()
-
-    def first_step(p, carry):
-        store_mid(p)
-        return carry
-
-    lax.fori_loop(2, 8, first_step, 0)
     pack_sides(mid, 4, y_send2, z_send2)
     sides = exchange_yz(y_send2, y_recv2, z_send2, z_recv2, y2_s, y2_r, z2_s, z2_r)
     for move in sides:
         move.start()
-    for move in sides:
-        move.wait()
-    unpack_sides(z_recv2, 4, halo_z)
-
-    def store_adv(p):
-        for c, x in enumerate(advance_plane(mid, visc, y_recv2, y_recv, halo_z, p)):
-            adv[c, p - 1] = x
-
-    def second_step(p, carry):
-        store_adv(p)
-        return carry
-
-    lax.fori_loop(2, 8, second_step, 0)
-    for move in moves:
-        move.wait()
-    store_adv(1)
-    store_adv(8)
-    write = pltpu.make_async_copy(adv, adv_hbm, local_sem.at[5])
-    write.start()
-
-    row = iota((128, 256), 0)
-    base = by_lane([(s // 256) * 128 + (s // 32 % 8) * 4 for s in picked], row // 16)
-    want = base + row // 4 % 4 * 32 + row % 4
-    hot = jnp.where(want == iota((128, 256), 1), 1.0, 0.0).astype(BF16)
-    lanes128 = iota((128, 128), 1)
-    keep = by_lane([s % 32 for s in picked], iota((128, 128), 0) // 16) == lanes128 // 4
+
+    def store_adv(p, out):
+        for c in range(4):
+            adv[c, p - 1] = out[c]
+
+    inner_part(mid, visc, store_adv)
     frow = iota((64, 128), 0)
     flane = iota((64, 128), 1)
     comp = frow % 4
-    zrow = frow // 4
     for i, c in enumerate(PAIR_P + PAIR_Q):
         here = (frow >= 16 + 4 * i) & (frow < 20 + 4 * i)
         comp = jnp.where(here, c, comp)
-    zrow = jnp.where(frow < 16, zrow, frow % 4)
+    zrow = jnp.where(frow < 16, frow // 4, frow % 4)
+    for c in range(4):
+        folds[c] = jnp.where((comp == c) & (flane % 4 == zrow), 1.0, 0.0).astype(BF16)
+    for load in loads[4:]:
+        load.wait()
+    st1[...] = jnp.zeros_like(st1)
+    st2[...] = jnp.zeros_like(st2)
+    for t in range(7):
+        width = 128 if t < 6 else 96
+        turned = w2[:, 128 * t : 128 * t + width].astype(F32).T
+        w2_turned[128 * t : 128 * t + width, :] = turned.astype(BF16)
+    pick_row = jnp.where(iota((24, 6), 0) // 4 == iota((24, 6), 1), 1.0, 0.0).astype(BF16)
+    pick_col = jnp.where(iota((32, 128), 1) % 32 == iota((32, 128), 0), 1.0, 0.0).astype(BF16)
+    spread3 = dot(dot(pick_row, w3[...]).astype(BF16), pick_col)
+    same_z = iota((24, 128), 0) % 4 == iota((24, 128), 1) // 32
+    wide3 = jnp.where(same_z, spread3, 0.0).astype(BF16)
+    all_here(t_send, t_recv, t_s, t_r, ay, in_y)
+    owned = t_recv[:, 0, :]
+    mine = by_lane(owners, iota((16, 128), 1) // 16)
+    load = jnp.zeros((16, 128), F32)
+    for s in range(8):
+        other_owner = owned if s == 0 else pltpu.roll(owned, s, 1)
+        load = load + jnp.where(other_owner == mine, 1.0, 0.0)
+    load = jnp.sum(load, axis=0, keepdims=True)
+    share = 1.0 / (WORKERS * jnp.maximum(load, 1.0))
+    scale = share * (2.0 / 384.0)
+    for move in moves:
+        move.wait()
+    for move in sides:
+        move.wait()
+    edge_part(
+        mid, visc, adv, 0, y_send2, y_recv2, (y_send, y_recv), z_send2, z_recv2, (z_send, z_recv)
+    )
+    write = pltpu.make_async_copy(adv, adv_hbm, local_sem.at[7])
+    write.start()
+
     cells = jnp.zeros((64, 128), F32)
     for c in range(4):
         plane = adv[c].reshape(256, 128).astype(BF16)
-        found = jnp.where(keep, dot(hot, plane), 0.0).astype(BF16)
-        fold = jnp.where((comp == c) & (flane % 4 == zrow), 1.0, 0.0).astype(BF16)
-        cells = cells + dot(fold, found, NT)
-
-    loads[2].wait()
-    loads[3].wait()
-    loads[4].wait()
-    st1[...] = jnp.zeros_like(st1)
+        found = (dot(hot[...], plane) * keep[...]).astype(BF16)
+        cells = cells + dot(folds[c], found, NT)
+
     chosen = cells[0:16]
     for i, (ox, oy) in enumerate(shifts()):
         moved = rolled(chosen, ox, oy)
@@ -338,39 +370,18 @@
             k = 3 * i + o
             for z in range(4):
                 if 0 <= z + o - 1 < 4:
-                    piece = moved[32 * (z + o - 1) : 32 * (z + o)]
-                else:
-                    piece = jnp.zeros((32, 128), BF16)
-                st2[32 * k : 32 * k + 32, 128 * z : 128 * z + 128] = piece
+                    st2[32 * k : 32 * k + 32, 128 * z : 128 * z + 128] = moved[
+                        32 * (z + o - 1) : 32 * (z + o)
+                    ]
     pre2 = cat_rows(dot(w2[...], st2[0:864, :]))
     sig2 = jax.nn.sigmoid(pre2)
     slope2 = sig2 * (1.0 + pre2 * (1.0 - sig2))
     hid2 = (pre2 * sig2).astype(BF16)
-    pick_row = jnp.where(iota((24, 6), 0) // 4 == iota((24, 6), 1), 1.0, 0.0).astype(BF16)
-    pick_col = jnp.where(iota((32, 128), 1) % 32 == iota((32, 128), 0), 1.0, 0.0).astype(BF16)
-    spread3 = dot(dot(pick_row, w3[...]).astype(BF16), pick_col)
-    same_z = iota((24, 128), 0) % 4 == iota((24, 128), 1) // 32
-    wide3 = jnp.where(same_z, spread3, 0.0).astype(BF16)
     predicted = dot(wide3, hid2)
     up_p, up_q = cells[16:40], cells[40:64]
-    target = box(up_p * up_q) - box(up_p) * box(up_q)
-    misfit = predicted - target
-
-    squares = jnp.broadcast_to(jnp.sum(misfit * misfit, axis=0, keepdims=True), (8, 128))
-    group = jnp.where(iota((128, 128), 0) // 16 == lanes128 % 8, 1.0, 0.0)
-    l_send[...] = dot(squares, group, precision=HIGH)[0:1] / 384.0
-    all_here(t_send, t_recv, t_s, t_r, ay, in_y)
-    everyone(l_send, l_recv, l_s, l_r, ay, in_y)
-    l_recv[ay] = l_send[...]
-    owned = t_recv[:, 0, :]
-    mine = by_lane(owners, iota((16, 128), 1) // 16)
-    load = jnp.zeros((16, 128), F32)
-    for s in range(8):
-        other_owner = owned if s == 0 else pltpu.roll(owned, s, 1)
-        load = load + jnp.where(other_owner == mine, 1.0, 0.0)
-    load = jnp.sum(load, axis=0, keepdims=True)
-    share = 1.0 / (WORKERS * jnp.maximum(load, 1.0))
-    grad_pred = (misfit * (share * (2.0 / 384.0))).astype(BF16)
+    smooth = box(jnp.concatenate([up_p * up_q, up_p, up_q], axis=0))
+    misfit = predicted - (smooth[0:24] - smooth[24:48] * smooth[48:72])
+    grad_pred = (misfit * scale).astype(BF16)
 
     third = jnp.where(same_z, dot(grad_pred, hid2, NT), 0.0)
     third = jnp.concatenate(
@@ -406,7 +417,7 @@
         send_tile(i)
     lower = jnp.zeros((128, 128), F32)
     for i, (ox, oy) in enumerate(shifts()):
-        y = dot(w2[:, 96 * i : 96 * i + 96], mid_cols, TN)
+        y = dot(w2_turned[96 * i : 96 * i + 96, :], mid_cols)
         parts = []
         for z in range(4):
             total = y[32:64, 128 * z : 128 * z + 128]
@@ -420,6 +431,12 @@
     entry_cols = jnp.concatenate([entry[32 * z : 32 * z + 32] for z in range(4)], axis=1)
     store_tile(7, dot(entry_cols, st1[...].astype(BF16), NT))
     send_tile(7)
+
+    squares = jnp.broadcast_to(jnp.sum(misfit * misfit, axis=0, keepdims=True), (8, 128))
+    group = jnp.where(iota((128, 128), 0) // 16 == lanes128 % 8, 1.0, 0.0)
+    l_send[...] = dot(squares, group, precision=HIGH)[0:1] / 384.0
+    everyone(l_send, l_recv, l_s, l_r, ay, in_y)
+    l_recv[ay] = l_send[...]
 
     part[aw] = grads[aw]
     for to in range(16):
@@ -454,13 +471,13 @@
         value = jnp.sum(jnp.where(own & (rank == r), losses, 0.0), axis=1, keepdims=True)
         slots = slots + jnp.where(place == r, value, 0.0)
     loss_out[...] = jnp.sum(slots, axis=0, keepdims=True)[:, 0:32]
-    write_loss = pltpu.make_async_copy(loss_out, loss_hbm, local_sem.at[6])
+    write_loss = pltpu.make_async_copy(loss_out, loss_hbm, local_sem.at[8])
     write_loss.start()
 
     all_here(sum1, spread, b_s, b_r, ay, in_y)
     sum2[...] = added(spread)
     everyone(sum2, final, c_s, c_r, aw, in_w)
-    own_part = pltpu.make_async_copy(sum2, final.at[aw], local_sem.at[7])
+    own_part = pltpu.make_async_copy(sum2, final.at[aw], local_sem.at[9])
     own_part.start()
     write.wait()
     write_loss.wait()
@@ -504,7 +521,6 @@
 
 
 def on_device(fields, viscosity, samples, trainers, conv_first, conv_second, conv_third):
-    smem = pl.BlockSpec(memory_space=pltpu.SMEM)
     hbm = pl.BlockSpec(memory_space=pl.ANY)
     dma = pltpu.SemaphoreType.DMA
     v = pltpu.VMEM
@@ -518,21 +534,22 @@
     results = pl.pallas_call(
         whole_kernel,
         out_shape=(shapes[0], shapes[1], jax.ShapeDtypeStruct((16, 16, 128), F32)),
-        in_specs=[hbm, hbm, smem, smem, hbm, hbm, hbm],
+        in_specs=[hbm] * 7,
         out_specs=(hbm,) * 3,
         scratch_shapes=[
+            pltpu.SMEM((8,), I32), pltpu.SMEM((8,), I32),
             v((5, 10, 32, 128), F32), v((4, 10, 32, 128), F32), v((4, 8, 32, 128), F32),
             v((2, 5, 8, 128), F32), v((2, 5, 8, 128), F32),
             v((2, 16, 128), F32), v((2, 16, 128), F32),
             v((2, 4, 8, 128), F32), v((2, 4, 8, 128), F32),
             v((2, 8, 128), F32), v((2, 8, 128), F32),
-            v((5, 8, 32, 128), F32),
             v((1, 128), I32), v((16, 1, 128), I32), v((1, 128), F32), v((16, 1, 128), F32),
             v((32, 108), BF16), v((32, 864), BF16), v((6, 32), BF16),
+            v((864, 32), BF16), v((128, 256), BF16), v((128, 128), F32), v((4, 64, 128), BF16),
             v((128, 512), F32), v((864, 512), BF16),
             v((16, 16, 128), F32), v((16, 16, 128), F32), v((16, 128), F32),
             v((16, 16, 128), F32), v((16, 128), F32), v((1, 32), F32),
-            dma((8,)),
+            dma((10,)),
             dma((2,)), dma((2,)), dma((2,)), dma((2,)), dma, dma,
             dma((2,)), dma((2,)), dma((2,)), dma((2,)), dma, dma,
             dma((16,)), dma((16,)), dma((16,)), dma((16,)),

time: 45.3 us -> 40.8 us (0.901)
  Pallas kernels: 44.5 us -> 40 us
    pallas_call x1, Pallas kernels: 42.6 us -> 38.1 us  [on_device(): pl.pallas_call(whole_kernel, out_shape=(shapes[0], shapes[1], jax.ShapeDt...]
where the time goes in v2:
time: 40.8 us; the launch traced here: 40.7 us
  Pallas kernels  40 us (98%)
  between operations  0.64 us (2%)
    pallas_call x1, Pallas kernels, on_device(): pl.pallas_call(whole_kernel, out_shape=(shapes[0], shapes[1], jax.ShapeDt...  38.1 us
    pallas_call x1, Pallas kernels, on_device(): pl.pallas_call(hand_over_kernel, out_shape=shapes, in_specs=[hbm] * 3, ou...  1.94 us

profile of v2, /device:TPU:1, one launch (start us, length us, event | category | flops | bytes accessed | tf_op | source)
XLA Modules:
  0.0 40.7 jit_solution(14060852543802879258)
XLA Ops:
  0.6 38.1 %step.1 = (f32[4,8,32,128]{3,2,1,0:T(8,128)}, f32[1,32]{1,0:T(1,128)}, f32[16,16,128]{2,1,0:T(8,128)}) custom-call(f32[4,8,32,128]{3,2,1,0:T(8,128)} %fields_hbm.1, f32[8,32,128]{2,1,0:T(8,128)} %visc_hbm.1, s32[8]{0:T(128)} %bitcast.3, s32[8]{0:T(128)} %bitcast.4, bf16[32,108]{1,0:T(8,128)(2,1)} %w1_hbm.1, bf16[32,864]{1,0:T(8,128)(2,1)} %w2_hbm.1, ...), custom_call_target="tpu_custom_call" | custom-call | tf_op jit(solution)/shard_map/step/pallas_call | solution.py:534
  38.7 1.9 %hand_over.1 = (f32[4,8,32,128]{3,2,1,0:T(8,128)}, f32[1,32]{1,0:T(1,128)}, f32[32,108]{1,0:T(8,128)}, f32[32,864]{1,0:T(8,128)}, f32[6,32]{1,0:T(8,128)}) custom-call(f32[4,8,32,128]{3,2,1,0:T(8,128)} %get-tuple-element.13.adv_in, f32[1,32]{1,0:T(1,128)} %get-tuple-element.14.loss_in, f32[16,16,128]{2,1,0:T(8,128)} %get-tuple-element.15.final_in), custom_call_target="tpu_custom_call" | custom-call | tf_op jit(solution)/shard_map/hand_over/pallas_call | solution.py:566

commit v3 on v2

--- a/solution.py
+++ b/solution.py
@@ -61,15 +61,14 @@
     plane(8, before, True)
 
 
-def edge_part(src, visc, dst, first, y_own, y_far, y_visc, z_own, z_far, z_visc):
+def edge_z(dst, first, z_own, z_far, v_own, v_far):
     rows = iota((128, 128), 0)
-    own_low = [z_own[0, 2 * c : 2 * c + 2] for c in range(4)]
-    own_high = [z_own[1, 2 * c : 2 * c + 2] for c in range(4)]
-    far_low = [z_far[0, 2 * c : 2 * c + 2] for c in range(4)]
-    far_high = [z_far[1, 2 * c : 2 * c + 2] for c in range(4)]
-    (v_own, v_far) = z_visc
-    low = flux(far_high, own_low, v_far[1, 8:10], v_own[0, 8:10], 2)
-    high = flux(own_high, far_low, v_own[1, 8:10], v_far[0, 8:10], 2)
+
+    def face(ref, side):
+        return [ref[side, 2 * c : 2 * c + 2] for c in range(4)]
+
+    low = flux(face(z_far, 1), face(z_own, 0), v_far[1, 8:10], v_own[0, 8:10], 2)
+    high = flux(face(z_own, 1), face(z_far, 0), v_own[1, 8:10], v_far[0, 8:10], 2)
     for c in range(4):
         for h in range(2):
             placed = jnp.where(
@@ -79,8 +78,20 @@
             )
             planes = slice(first + 4 * h, first + 4 * h + 4)
             dst[c, planes] = dst[c, planes] + placed.T.reshape(4, 32, 128)
-    (v_own, v_far) = y_visc
-
+
+
+def edge_x(src, visc, dst, first):
+    def of(p):
+        return [src[c, p] for c in range(4)]
+
+    low = flux(of(0), of(1), visc(0), visc(1), 0)
+    high = flux(of(8), of(9), visc(8), visc(9), 0)
+    for c in range(4):
+        dst[c, first] = dst[c, first] + TIME_STEP * low[c]
+        dst[c, first + 7] = dst[c, first + 7] - TIME_STEP * high[c]
+
+
+def edge_y(dst, first, y_own, y_far, v_own, v_far):
     def face(ref, side):
         return [ref[side, c] for c in range(4)]
 
@@ -91,20 +102,15 @@
         dst[c, planes, 0, :] = dst[c, planes, 0, :] + TIME_STEP * low[c]
         dst[c, planes, 31, :] = dst[c, planes, 31, :] - TIME_STEP * high[c]
 
-    def of(p):
-        return [src[c, p] for c in range(4)]
-
-    low = flux(of(0), of(1), visc(0), visc(1), 0)
-    high = flux(of(8), of(9), visc(8), visc(9), 0)
-    for c in range(4):
-        dst[c, first] = dst[c, first] + TIME_STEP * low[c]
-        dst[c, first + 7] = dst[c, first + 7] - TIME_STEP * high[c]
-
-
-def pack_sides(src, count, y_send, z_send):
+
+def pack_y(src, count, y_send):
     for c in range(count):
         y_send[0, c] = src[c, 1:9, 0, :]
         y_send[1, c] = src[c, 1:9, 31, :]
+
+
+def pack_z(src, count, z_send):
+    for c in range(count):
         for h in range(2):
             turned = src[c, 1 + 4 * h : 5 + 4 * h].reshape(128, 128).T
             g = 2 * c + h
@@ -177,14 +183,20 @@
     ax = lax.axis_index("gx")
     ay = lax.axis_index("gy")
     az = lax.axis_index("gz")
-    aw = ax * NZ + az
+    half = ay // 8
+    az_seen = lax.rem(az + half, 2)
+    aw = ax * NZ + az_seen
+
+    def in_same(d):
+        to = lax.rem(ay + d, NY)
+        return (ax, to, lax.rem(az_seen + to // 8, 2))
 
     def in_y(d):
         return (ax, lax.rem(ay + d, NY), az)
 
     def in_w(d):
         w = lax.rem(aw + d, NX * NZ)
-        return (w // NZ, ay, lax.rem(w, NZ))
+        return (w // NZ, ay, lax.rem(w + half, NZ))
 
     loads = [
         pltpu.make_async_copy(src, dst, local_sem.at[i])
@@ -210,15 +222,23 @@
         return carry
 
     lax.fori_loop(1, 16, greet, 0)
+
+    def greet_mirrored(d, carry):
+        to = lax.rem((1 - half) * 8 + d, NY)
+        pl.semaphore_signal(barrier, inc=1, device_id=(ax, to, 1 - az), device_id_type=MESH)
+        return carry
+
+    lax.fori_loop(0, 8, greet_mirrored, 0)
     for load in loads[2:]:
         load.start()
     loads[0].wait()
     loads[1].wait()
-    pack_sides(start, 5, y_send, z_send)
+    pack_y(start, 5, y_send)
+    pack_z(start, 5, z_send)
     loads[2].wait()
     owners = [trainers[j] for j in range(8)]
     t_send[...] = by_lane(owners, iota((1, 128), 1) % 8)
-    pl.semaphore_wait(barrier, 30)
+    pl.semaphore_wait(barrier, 38)
 
     def remote(src, dst, s, r, to):
         return pltpu.make_async_remote_copy(
@@ -235,34 +255,43 @@
             remote(ref.at[:, 1], ref.at[:, 9], s.at[1], r.at[1], x_down),
         ]
 
-    def exchange_yz(ys, yr, zs, zr, ysem, yrem, zsem, zrem):
+    def exchange_y(ys, yr, s, r):
         return [
-            remote(ys.at[1], yr.at[0], ysem.at[0], yrem.at[0], in_y(1)),
-            remote(ys.at[0], yr.at[1], ysem.at[1], yrem.at[1], in_y(NY - 1)),
-            remote(zs, zr, zsem, zrem, other),
+            remote(ys.at[1], yr.at[0], s.at[0], r.at[0], in_y(1)),
+            remote(ys.at[0], yr.at[1], s.at[1], r.at[1], in_y(NY - 1)),
         ]
 
+    def begin(moves):
+        for move in moves:
+            move.start()
+
+    def finish(moves):
+        for move in moves:
+            move.wait()
+
     def everyone(src, buf, s, r, slot, to):
-        def begin(d, carry):
+        def send(d, carry):
             remote(src, buf.at[slot], s.at[d], r.at[slot], to(d)).start()
             return carry
 
-        lax.fori_loop(1, 16, begin, 0)
+        lax.fori_loop(1, 16, send, 0)
 
     def all_here(src, buf, s, r, slot, to):
-        def finish(d, carry):
+        def receive(d, carry):
             at = lax.rem(slot + d, 16)
             copy = remote(src, buf.at[at], s.at[d], r.at[at], to(d))
             copy.wait_send()
             copy.wait_recv()
             return carry
 
-        lax.fori_loop(1, 16, finish, 0)
-
-    moves = exchange_x(start, x_s, x_r)
-    moves += exchange_yz(y_send, y_recv, z_send, z_recv, y_s, y_r, z_s, z_r)
-    for move in moves:
-        move.start()
+        lax.fori_loop(1, 16, receive, 0)
+
+    moves_y = exchange_y(y_send, y_recv, y_s, y_r)
+    moves_x = exchange_x(start, x_s, x_r)
+    moves_z = [remote(z_send, z_recv, z_s, z_r, other)]
+    begin(moves_y)
+    begin(moves_x)
+    begin(moves_z)
     everyone(t_send, t_recv, t_s, t_r, ay, in_y)
     t_recv[ay] = t_send[...]
 
@@ -283,19 +312,21 @@
     lanes128 = iota((128, 128), 1)
     lz = by_lane([s % 32 for s in picked], iota((128, 128), 0) // 16)
     keep[...] = jnp.where(lz == lanes128 // 4, 1.0, 0.0)
-    for move in moves:
-        move.wait()
-    edge_part(
-        start, visc, mid, 1, y_send, y_recv, (y_send, y_recv), z_send, z_recv, (z_send, z_recv)
-    )
-
-    moves = exchange_x(mid, x2_s, x2_r)
-    for move in moves:
-        move.start()
-    pack_sides(mid, 4, y_send2, z_send2)
-    sides = exchange_yz(y_send2, y_recv2, z_send2, z_recv2, y2_s, y2_r, z2_s, z2_r)
-    for move in sides:
-        move.start()
+    finish(moves_z)
+    edge_z(mid, 1, z_send, z_recv, z_send, z_recv)
+    finish(moves_x)
+    edge_x(start, visc, mid, 1)
+    finish(moves_y)
+    edge_y(mid, 1, y_send, y_recv, y_send, y_recv)
+
+    pack_y(mid, 4, y_send2)
+    moves_y = exchange_y(y_send2, y_recv2, y2_s, y2_r)
+    begin(moves_y)
+    moves_x = exchange_x(mid, x2_s, x2_r)
+    begin(moves_x)
+    pack_z(mid, 4, z_send2)
+    moves_z = [remote(z_send2, z_recv2, z2_s, z2_r, other)]
+    begin(moves_z)
 
     def store_adv(p, out):
         for c in range(4):
@@ -334,13 +365,12 @@
     load = jnp.sum(load, axis=0, keepdims=True)
     share = 1.0 / (WORKERS * jnp.maximum(load, 1.0))
     scale = share * (2.0 / 384.0)
-    for move in moves:
-        move.wait()
-    for move in sides:
-        move.wait()
-    edge_part(
-        mid, visc, adv, 0, y_send2, y_recv2, (y_send, y_recv), z_send2, z_recv2, (z_send, z_recv)
-    )
+    finish(moves_z)
+    edge_z(adv, 0, z_send2, z_recv2, z_send, z_recv)
+    finish(moves_x)
+    edge_x(mid, visc, adv, 0)
+    finish(moves_y)
+    edge_y(adv, 0, y_send2, y_recv2, y_send, y_recv)
     write = pltpu.make_async_copy(adv, adv_hbm, local_sem.at[7])
     write.start()
 
@@ -401,12 +431,12 @@
             @pl.when(aw != to)
             def _():
                 remote(
-                    grads.at[to], part.at[aw], a_s.at[to], a_r.at[aw], (to // NZ, ay, to % NZ)
+                    grads.at[to], part.at[aw], a_s.at[to], a_r.at[aw], (to // NZ, ay, lax.rem(to + half, NZ))
                 ).start()
 
     def store_tile(i, x):
-        grads[2 * i] = x[0:16]
-        grads[2 * i + 1] = x[16:32]
+        grads[2 * i] = x[0:16].astype(BF16)
+        grads[2 * i + 1] = x[16:32].astype(BF16)
 
     for i in range(7):
         rows_here = 128 if i < 6 else 96
@@ -444,17 +474,17 @@
         @pl.when(aw != to)
         def _():
             remote(
-                grads.at[to], part.at[to], a_s.at[to], a_r.at[to], (to // NZ, ay, to % NZ)
+                grads.at[to], part.at[to], a_s.at[to], a_r.at[to], (to // NZ, ay, lax.rem(to + half, NZ))
             ).wait()
 
     def added(buf):
-        total = buf[0]
+        total = buf[0].astype(F32)
         for s in range(1, 16):
-            total = total + buf[s]
+            total = total + buf[s].astype(F32)
         return total
 
-    sum1[...] = added(part)
-    everyone(sum1, spread, b_s, b_r, ay, in_y)
+    sum1[...] = added(part).astype(BF16)
+    everyone(sum1, spread, b_s, b_r, ay, in_same)
     spread[ay] = sum1[...]
 
     all_here(l_send, l_recv, l_s, l_r, ay, in_y)
@@ -474,8 +504,8 @@
     write_loss = pltpu.make_async_copy(loss_out, loss_hbm, local_sem.at[8])
     write_loss.start()
 
-    all_here(sum1, spread, b_s, b_r, ay, in_y)
-    sum2[...] = added(spread)
+    all_here(sum1, spread, b_s, b_r, ay, in_same)
+    sum2[...] = added(spread).astype(BF16)
     everyone(sum2, final, c_s, c_r, aw, in_w)
     own_part = pltpu.make_async_copy(sum2, final.at[aw], local_sem.at[9])
     own_part.start()
@@ -489,32 +519,36 @@
     adv_in, loss_in, final_in, adv_out, loss_out, first_out, second_out, third_out,
     adv, loss, final, first, second, third, sem,
 ):
-    loads = [pltpu.make_async_copy(adv_in.at[c], adv.at[c], sem.at[c]) for c in range(4)]
-    loads.append(pltpu.make_async_copy(loss_in, loss, sem.at[4]))
     load_final = pltpu.make_async_copy(final_in, final, sem.at[5])
     load_final.start()
+    pieces = [(c, slice(4 * h, 4 * h + 4)) for c in range(4) for h in range(2)]
+    loads = [
+        pltpu.make_async_copy(adv_in.at[piece], adv.at[piece], sem.at[6 + i])
+        for i, piece in enumerate(pieces)
+    ]
+    loads.append(pltpu.make_async_copy(loss_in, loss, sem.at[4]))
     for load in loads:
         load.start()
     load_final.wait()
     for i in range(6):
-        second[:, 128 * i : 128 * i + 128] = final[2 * i : 2 * i + 2].reshape(32, 128)
-    last = final[12:14].reshape(32, 128)
+        second[:, 128 * i : 128 * i + 128] = final[2 * i : 2 * i + 2].astype(F32).reshape(32, 128)
+    last = final[12:14].astype(F32).reshape(32, 128)
     second[:, 768:864] = last[:, 0:96]
     third[...] = last[0:6, 96:128]
-    first[...] = final[14:16].reshape(32, 128)[:, 0:108]
+    first[...] = final[14:16].astype(F32).reshape(32, 128)[:, 0:108]
     stores = [
-        pltpu.make_async_copy(second, second_out, sem.at[6]),
-        pltpu.make_async_copy(first, first_out, sem.at[7]),
-        pltpu.make_async_copy(third, third_out, sem.at[8]),
+        pltpu.make_async_copy(second, second_out, sem.at[0]),
+        pltpu.make_async_copy(first, first_out, sem.at[1]),
+        pltpu.make_async_copy(third, third_out, sem.at[2]),
     ]
     for store in stores:
         store.start()
-    for c in range(4):
-        loads[c].wait()
-        stores.append(pltpu.make_async_copy(adv.at[c], adv_out.at[c], sem.at[9 + c]))
+    for i, piece in enumerate(pieces):
+        loads[i].wait()
+        stores.append(pltpu.make_async_copy(adv.at[piece], adv_out.at[piece], sem.at[14 + i]))
         stores[-1].start()
-    loads[4].wait()
-    stores.append(pltpu.make_async_copy(loss, loss_out, sem.at[13]))
+    loads[8].wait()
+    stores.append(pltpu.make_async_copy(loss, loss_out, sem.at[3]))
     stores[-1].start()
     for store in stores:
         store.wait()
@@ -533,7 +567,7 @@
     )
     results = pl.pallas_call(
         whole_kernel,
-        out_shape=(shapes[0], shapes[1], jax.ShapeDtypeStruct((16, 16, 128), F32)),
+        out_shape=(shapes[0], shapes[1], jax.ShapeDtypeStruct((16, 16, 128), BF16)),
         in_specs=[hbm] * 7,
         out_specs=(hbm,) * 3,
         scratch_shapes=[
@@ -547,8 +581,8 @@
             v((32, 108), BF16), v((32, 864), BF16), v((6, 32), BF16),
             v((864, 32), BF16), v((128, 256), BF16), v((128, 128), F32), v((4, 64, 128), BF16),
             v((128, 512), F32), v((864, 512), BF16),
-            v((16, 16, 128), F32), v((16, 16, 128), F32), v((16, 128), F32),
-            v((16, 16, 128), F32), v((16, 128), F32), v((1, 32), F32),
+            v((16, 16, 128), BF16), v((16, 16, 128), BF16), v((16, 128), BF16),
+            v((16, 16, 128), BF16), v((16, 128), BF16), v((1, 32), F32),
             dma((10,)),
             dma((2,)), dma((2,)), dma((2,)), dma((2,)), dma, dma,
             dma((2,)), dma((2,)), dma((2,)), dma((2,)), dma, dma,
@@ -569,8 +603,8 @@
         in_specs=[hbm] * 3,
         out_specs=(hbm,) * 5,
         scratch_shapes=[
-            v((4, 8, 32, 128), F32), v((1, 32), F32), v((16, 16, 128), F32),
-            v((32, 108), F32), v((32, 864), F32), v((6, 32), F32), dma((14,)),
+            v((4, 8, 32, 128), F32), v((1, 32), F32), v((16, 16, 128), BF16),
+            v((32, 108), F32), v((32, 864), F32), v((6, 32), F32), dma((22,)),
         ],
         compiler_params=pltpu.CompilerParams(vmem_limit_bytes=60 * 1024 * 1024),
         name="hand_over",

time: 40.8 us -> 39.1 us (0.958)
  Pallas kernels: 40 us -> 38.3 us
    pallas_call x1, Pallas kernels: 38.1 us -> 36.3 us  [on_device(): pl.pallas_call(whole_kernel, out_shape=(shapes[0], shapes[1], jax.ShapeDt...]
where the time goes in v3:
time: 39.1 us; the launch traced here: 38.9 us
  Pallas kernels  38.3 us (98%)
  between operations  0.64 us (2%)
    pallas_call x1, Pallas kernels, on_device(): pl.pallas_call(whole_kernel, out_shape=(shapes[0], shapes[1], jax.ShapeDt...  36.3 us
    pallas_call x1, Pallas kernels, on_device(): pl.pallas_call(hand_over_kernel, out_shape=shapes, in_specs=[hbm] * 3, ou...  1.92 us

profile of v3, /device:TPU:1, one launch (start us, length us, event | category | flops | bytes accessed | tf_op | source)
XLA Modules:
  0.0 38.9 jit_solution(14758014271271892215)
XLA Ops:
  0.6 36.3 %step.1 = (f32[4,8,32,128]{3,2,1,0:T(8,128)}, f32[1,32]{1,0:T(1,128)}, bf16[16,16,128]{2,1,0:T(8,128)(2,1)}) custom-call(f32[4,8,32,128]{3,2,1,0:T(8,128)} %fields_hbm.1, f32[8,32,128]{2,1,0:T(8,128)} %visc_hbm.1, s32[8]{0:T(128)} %bitcast.3, s32[8]{0:T(128)} %bitcast.4, bf16[32,108]{1,0:T(8,128)(2,1)} %w1_hbm.1, bf16[32,864]{1,0:T(8,128)(2,1)} %w2_hbm.1, ...), custom_call_target="tpu_custom_call" | custom-call | tf_op jit(solution)/shard_map/step/pallas_call | solution.py:568
  37.0 1.9 %hand_over.1 = (f32[4,8,32,128]{3,2,1,0:T(8,128)}, f32[1,32]{1,0:T(1,128)}, f32[32,108]{1,0:T(8,128)}, f32[32,864]{1,0:T(8,128)}, f32[6,32]{1,0:T(8,128)}) custom-call(f32[4,8,32,128]{3,2,1,0:T(8,128)} %get-tuple-element.13.adv_in, f32[1,32]{1,0:T(1,128)} %get-tuple-element.14.loss_in, bf16[16,16,128]{2,1,0:T(8,128)(2,1)} %get-tuple-element.15.final_in), custom_call_target="tpu_custom_call" | custom-call | tf_op jit(solution)/shard_map/hand_over/pallas_call | solution.py:600

commit v4 on v3

--- a/solution.py
+++ b/solution.py
@@ -17,6 +17,8 @@
 TN = (((0,), (0,)), ((), ()))
 TIME_STEP = 0.25
 BUOYANCY = 0.5
+FAR_Y = (4, 12, 3, 5, 11, 13, 2, 6, 10, 14, 1, 7, 9, 15, 8)
+FAR_W = (8, 9, 10, 7, 11, 6, 5, 4, 12, 13, 14, 3, 2, 15, 1)
 PAIR_P = (0, 1, 2, 0, 0, 1)
 PAIR_Q = (0, 1, 2, 1, 2, 2)
 
@@ -269,22 +271,17 @@
         for move in moves:
             move.wait()
 
-    def everyone(src, buf, s, r, slot, to):
-        def send(d, carry):
-            remote(src, buf.at[slot], s.at[d], r.at[slot], to(d)).start()
-            return carry
-
-        lax.fori_loop(1, 16, send, 0)
-
-    def all_here(src, buf, s, r, slot, to):
-        def receive(d, carry):
-            at = lax.rem(slot + d, 16)
-            copy = remote(src, buf.at[at], s.at[d], r.at[at], to(d))
-            copy.wait_send()
-            copy.wait_recv()
-            return carry
-
-        lax.fori_loop(1, 16, receive, 0)
+    def everyone(src, buf, s, r, slot, to, order):
+        for d in order:
+            remote(src, buf.at[slot], s, r, to(d)).start()
+
+    def all_here(buf, s, r):
+        others = buf.at[pl.ds(0, 15)]
+        remote(others, others, s, r, other).wait_recv()
+
+    def all_sent(buf, s, r):
+        others = buf.at[pl.ds(0, 15)]
+        remote(others, others, s, r, other).wait_send()
 
     moves_y = exchange_y(y_send, y_recv, y_s, y_r)
     moves_x = exchange_x(start, x_s, x_r)
@@ -292,7 +289,7 @@
     begin(moves_y)
     begin(moves_x)
     begin(moves_z)
-    everyone(t_send, t_recv, t_s, t_r, ay, in_y)
+    everyone(t_send, t_recv, t_s, t_r, ay, in_y, FAR_Y)
     t_recv[ay] = t_send[...]
 
     def visc(p):
@@ -355,7 +352,7 @@
     spread3 = dot(dot(pick_row, w3[...]).astype(BF16), pick_col)
     same_z = iota((24, 128), 0) % 4 == iota((24, 128), 1) // 32
     wide3 = jnp.where(same_z, spread3, 0.0).astype(BF16)
-    all_here(t_send, t_recv, t_s, t_r, ay, in_y)
+    all_here(t_recv, t_s, t_r)
     owned = t_recv[:, 0, :]
     mine = by_lane(owners, iota((16, 128), 1) // 16)
     load = jnp.zeros((16, 128), F32)
@@ -431,7 +428,7 @@
             @pl.when(aw != to)
             def _():
                 remote(
-                    grads.at[to], part.at[aw], a_s.at[to], a_r.at[aw], (to // NZ, ay, lax.rem(to + half, NZ))
+                    grads.at[to], part.at[aw], a_s, a_r, (to // NZ, ay, lax.rem(to + half, NZ))
                 ).start()
 
     def store_tile(i, x):
@@ -465,17 +462,11 @@
     squares = jnp.broadcast_to(jnp.sum(misfit * misfit, axis=0, keepdims=True), (8, 128))
     group = jnp.where(iota((128, 128), 0) // 16 == lanes128 % 8, 1.0, 0.0)
     l_send[...] = dot(squares, group, precision=HIGH)[0:1] / 384.0
-    everyone(l_send, l_recv, l_s, l_r, ay, in_y)
+    everyone(l_send, l_recv, l_s, l_r, ay, in_y, FAR_Y)
     l_recv[ay] = l_send[...]
 
     part[aw] = grads[aw]
-    for to in range(16):
-
-        @pl.when(aw != to)
-        def _():
-            remote(
-                grads.at[to], part.at[to], a_s.at[to], a_r.at[to], (to // NZ, ay, lax.rem(to + half, NZ))
-            ).wait()
+    all_here(part, a_s, a_r)
 
     def added(buf):
         total = buf[0].astype(F32)
@@ -484,10 +475,10 @@
         return total
 
     sum1[...] = added(part).astype(BF16)
-    everyone(sum1, spread, b_s, b_r, ay, in_same)
+    everyone(sum1, spread, b_s, b_r, ay, in_same, FAR_Y)
     spread[ay] = sum1[...]
 
-    all_here(l_send, l_recv, l_s, l_r, ay, in_y)
+    all_here(l_recv, l_s, l_r)
     lanes16 = iota((16, 128), 1)
     rank = jnp.zeros((16, 128), I32)
     for s in range(1, 8):
@@ -504,15 +495,20 @@
     write_loss = pltpu.make_async_copy(loss_out, loss_hbm, local_sem.at[8])
     write_loss.start()
 
-    all_here(sum1, spread, b_s, b_r, ay, in_same)
+    all_here(spread, b_s, b_r)
     sum2[...] = added(spread).astype(BF16)
-    everyone(sum2, final, c_s, c_r, aw, in_w)
+    everyone(sum2, final, c_s, c_r, aw, in_w, FAR_W)
     own_part = pltpu.make_async_copy(sum2, final.at[aw], local_sem.at[9])
     own_part.start()
     write.wait()
     write_loss.wait()
     own_part.wait()
-    all_here(sum2, final, c_s, c_r, aw, in_w)
+    for buf, s, r in (
+        (t_recv, t_s, t_r), (l_recv, l_s, l_r), (part, a_s, a_r), (spread, b_s, b_r),
+        (final, c_s, c_r),
+    ):
+        all_sent(buf, s, r)
+    all_here(final, c_s, c_r)
 
 
 def hand_over_kernel(
@@ -586,8 +582,7 @@
             dma((10,)),
             dma((2,)), dma((2,)), dma((2,)), dma((2,)), dma, dma,
             dma((2,)), dma((2,)), dma((2,)), dma((2,)), dma, dma,
-            dma((16,)), dma((16,)), dma((16,)), dma((16,)),
-            dma((16,)), dma((16,)), dma((16,)), dma((16,)), dma((16,)), dma((16,)),
+            dma, dma, dma, dma, dma, dma, dma, dma, dma, dma,
         ],
         compiler_params=pltpu.CompilerParams(
             collective_id=0, has_side_effects=True, vmem_limit_bytes=60 * 1024 * 1024

time: 39.1 us -> 38 us (0.972)
  Pallas kernels: 38.3 us -> 37.2 us
    pallas_call x1, Pallas kernels: 36.3 us -> 35.3 us  [on_device(): pl.pallas_call(whole_kernel, out_shape=(shapes[0], shapes[1], jax.ShapeDt...]
where the time goes in v4:
time: 38 us; the launch traced here: 37.8 us
  Pallas kernels  37.2 us (98%)
  between operations  0.64 us (2%)
    pallas_call x1, Pallas kernels, on_device(): pl.pallas_call(whole_kernel, out_shape=(shapes[0], shapes[1], jax.ShapeDt...  35.3 us
    pallas_call x1, Pallas kernels, on_device(): pl.pallas_call(hand_over_kernel, out_shape=shapes, in_specs=[hbm] * 3, ou...  1.92 us

profile of v4, /device:TPU:1, one launch (start us, length us, event | category | flops | bytes accessed | tf_op | source)
XLA Modules:
  0.0 37.8 jit_solution(10849990774580766982)
XLA Ops:
  0.6 35.3 %step.1 = (f32[4,8,32,128]{3,2,1,0:T(8,128)}, f32[1,32]{1,0:T(1,128)}, bf16[16,16,128]{2,1,0:T(8,128)(2,1)}) custom-call(f32[4,8,32,128]{3,2,1,0:T(8,128)} %fields_hbm.1, f32[8,32,128]{2,1,0:T(8,128)} %visc_hbm.1, s32[8]{0:T(128)} %bitcast.3, s32[8]{0:T(128)} %bitcast.4, bf16[32,108]{1,0:T(8,128)(2,1)} %w1_hbm.1, bf16[32,864]{1,0:T(8,128)(2,1)} %w2_hbm.1, ...), custom_call_target="tpu_custom_call" | custom-call | tf_op jit(solution)/shard_map/step/pallas_call | solution.py:564
  35.9 1.9 %hand_over.1 = (f32[4,8,32,128]{3,2,1,0:T(8,128)}, f32[1,32]{1,0:T(1,128)}, f32[32,108]{1,0:T(8,128)}, f32[32,864]{1,0:T(8,128)}, f32[6,32]{1,0:T(8,128)}) custom-call(f32[4,8,32,128]{3,2,1,0:T(8,128)} %get-tuple-element.13.adv_in, f32[1,32]{1,0:T(1,128)} %get-tuple-element.14.loss_in, bf16[16,16,128]{2,1,0:T(8,128)(2,1)} %get-tuple-element.15.final_in), custom_call_target="tpu_custom_call" | custom-call | tf_op jit(solution)/shard_map/hand_over/pallas_call | solution.py:595

commit v5 on v4

--- a/solution.py
+++ b/solution.py
@@ -421,27 +421,10 @@
     grad_mid = (dot(wide3, grad_pred, TN) * slope2).astype(BF16)
     mid_cols = jnp.concatenate([grad_mid[32 * z : 32 * z + 32] for z in range(4)], axis=1)
 
-    def send_tile(i):
-        for h in range(2):
-            to = 2 * i + h
-
-            @pl.when(aw != to)
-            def _():
-                remote(
-                    grads.at[to], part.at[aw], a_s, a_r, (to // NZ, ay, lax.rem(to + half, NZ))
-                ).start()
-
     def store_tile(i, x):
         grads[2 * i] = x[0:16].astype(BF16)
         grads[2 * i + 1] = x[16:32].astype(BF16)
 
-    for i in range(7):
-        rows_here = 128 if i < 6 else 96
-        tile = dot(mid_cols, st2[128 * i : 128 * i + rows_here, :], NT)
-        if i == 6:
-            tile = jnp.concatenate([tile, third[:, 96:128]], axis=1)
-        store_tile(i, tile)
-        send_tile(i)
     lower = jnp.zeros((128, 128), F32)
     for i, (ox, oy) in enumerate(shifts()):
         y = dot(w2_turned[96 * i : 96 * i + 96, :], mid_cols)
@@ -457,7 +440,15 @@
     entry = (lower * slope1).astype(BF16)
     entry_cols = jnp.concatenate([entry[32 * z : 32 * z + 32] for z in range(4)], axis=1)
     store_tile(7, dot(entry_cols, st1[...].astype(BF16), NT))
-    send_tile(7)
+    for i in range(7):
+        rows_here = 128 if i < 6 else 96
+        tile = dot(mid_cols, st2[128 * i : 128 * i + rows_here, :], NT)
+        if i == 6:
+            tile = jnp.concatenate([tile, third[:, 96:128]], axis=1)
+        store_tile(i, tile)
+    for d in FAR_W:
+        to = lax.rem(aw + d, NX * NZ)
+        remote(grads.at[to], part.at[aw], a_s, a_r, in_w(d)).start()
 
     squares = jnp.broadcast_to(jnp.sum(misfit * misfit, axis=0, keepdims=True), (8, 128))
     group = jnp.where(iota((128, 128), 0) // 16 == lanes128 % 8, 1.0, 0.0)

time: 38 us -> 37.4 us (0.984)
  Pallas kernels: 37.2 us -> 36.6 us
    pallas_call x1, Pallas kernels: 35.3 us -> 34.6 us  [on_device(): pl.pallas_call(whole_kernel, out_shape=(shapes[0], shapes[1], jax.ShapeDt...]
where the time goes in v5:
time: 37.4 us; the launch traced here: 37.2 us
  Pallas kernels  36.6 us (98%)
  between operations  0.64 us (2%)
    pallas_call x1, Pallas kernels, on_device(): pl.pallas_call(whole_kernel, out_shape=(shapes[0], shapes[1], jax.ShapeDt...  34.6 us
    pallas_call x1, Pallas kernels, on_device(): pl.pallas_call(hand_over_kernel, out_shape=shapes, in_specs=[hbm] * 3, ou...  1.92 us

profile of v5, /device:TPU:1, one launch (start us, length us, event | category | flops | bytes accessed | tf_op | source)
XLA Modules:
  0.0 37.2 jit_solution(757320389453432530)
XLA Ops:
  0.6 34.6 %step.1 = (f32[4,8,32,128]{3,2,1,0:T(8,128)}, f32[1,32]{1,0:T(1,128)}, bf16[16,16,128]{2,1,0:T(8,128)(2,1)}) custom-call(f32[4,8,32,128]{3,2,1,0:T(8,128)} %fields_hbm.1, f32[8,32,128]{2,1,0:T(8,128)} %visc_hbm.1, s32[8]{0:T(128)} %bitcast.3, s32[8]{0:T(128)} %bitcast.4, bf16[32,108]{1,0:T(8,128)(2,1)} %w1_hbm.1, bf16[32,864]{1,0:T(8,128)(2,1)} %w2_hbm.1, ...), custom_call_target="tpu_custom_call" | custom-call | tf_op jit(solution)/shard_map/step/pallas_call | solution.py:555
  35.3 1.9 %hand_over.1 = (f32[4,8,32,128]{3,2,1,0:T(8,128)}, f32[1,32]{1,0:T(1,128)}, f32[32,108]{1,0:T(8,128)}, f32[32,864]{1,0:T(8,128)}, f32[6,32]{1,0:T(8,128)}) custom-call(f32[4,8,32,128]{3,2,1,0:T(8,128)} %get-tuple-element.13.adv_in, f32[1,32]{1,0:T(1,128)} %get-tuple-element.14.loss_in, bf16[16,16,128]{2,1,0:T(8,128)(2,1)} %get-tuple-element.15.final_in), custom_call_target="tpu_custom_call" | custom-call | tf_op jit(solution)/shard_map/hand_over/pallas_call | solution.py:586

commit v6 on v5

--- a/solution.py
+++ b/solution.py
@@ -267,9 +267,12 @@
         for move in moves:
             move.start()
 
+    leaving = []
+
     def finish(moves):
         for move in moves:
-            move.wait()
+            move.wait_recv()
+        leaving.extend(moves)
 
     def everyone(src, buf, s, r, slot, to, order):
         for d in order:
@@ -499,6 +502,8 @@
         (final, c_s, c_r),
     ):
         all_sent(buf, s, r)
+    for move in leaving:
+        move.wait_send()
     all_here(final, c_s, c_r)
 
 

time: 37.4 us -> 37.4 us (level)
  no operation moved by 1% of the time
where the time goes in v6:
time: 37.4 us; the launch traced here: 37.2 us
  Pallas kernels  36.6 us (98%)
  between operations  0.64 us (2%)
    pallas_call x1, Pallas kernels, on_device(): pl.pallas_call(whole_kernel, out_shape=(shapes[0], shapes[1], jax.ShapeDt...  34.6 us
    pallas_call x1, Pallas kernels, on_device(): pl.pallas_call(hand_over_kernel, out_shape=shapes, in_specs=[hbm] * 3, ou...  1.92 us

profile of v6, /device:TPU:1, one launch (start us, length us, event | category | flops | bytes accessed | tf_op | source)
XLA Modules:
  0.0 37.2 jit_solution(17298368020017405544)
XLA Ops:
  0.6 34.6 %step.1 = (f32[4,8,32,128]{3,2,1,0:T(8,128)}, f32[1,32]{1,0:T(1,128)}, bf16[16,16,128]{2,1,0:T(8,128)(2,1)}) custom-call(f32[4,8,32,128]{3,2,1,0:T(8,128)} %fields_hbm.1, f32[8,32,128]{2,1,0:T(8,128)} %visc_hbm.1, s32[8]{0:T(128)} %bitcast.3, s32[8]{0:T(128)} %bitcast.4, bf16[32,108]{1,0:T(8,128)(2,1)} %w1_hbm.1, bf16[32,864]{1,0:T(8,128)(2,1)} %w2_hbm.1, ...), custom_call_target="tpu_custom_call" | custom-call | tf_op jit(solution)/shard_map/step/pallas_call | solution.py:560
  35.3 1.9 %hand_over.1 = (f32[4,8,32,128]{3,2,1,0:T(8,128)}, f32[1,32]{1,0:T(1,128)}, f32[32,108]{1,0:T(8,128)}, f32[32,864]{1,0:T(8,128)}, f32[6,32]{1,0:T(8,128)}) custom-call(f32[4,8,32,128]{3,2,1,0:T(8,128)} %get-tuple-element.13.adv_in, f32[1,32]{1,0:T(1,128)} %get-tuple-element.14.loss_in, bf16[16,16,128]{2,1,0:T(8,128)(2,1)} %get-tuple-element.15.final_in), custom_call_target="tpu_custom_call" | custom-call | tf_op jit(solution)/shard_map/hand_over/pallas_call | solution.py:591
